TPU v7x, 32 devices: a whole 2x2x4 slice. The times are simulated.
32 devices in a mesh: grp: 2 (over x), cuts: 16 (over z, y, core).
Axes of the slice: x: 2, y: 2, z: 4, core: 2. Of those that a mesh axis runs over, the one named last changes fastest.
Arguments:
- stem_tensor: bfloat16 [2, 128, 32, 512], P(None, ('grp', 'cuts')), parts along dimension 1
- branch_tensors: bfloat16 [2, 2, 2, 512, 512], replicated, may hold values from -0.1875 to 0.1875
- cut_values: int32 [128, 2], P(('grp', 'cuts')), parts along dimension 0, may hold values from 0 to 1
- bit_rows: int32 [16384], P('grp'), parts along dimension 0, may hold values from 0 to 31
- bit_cols: int32 [16384], P('grp'), parts along dimension 0, may hold values from 0 to 511
Outputs:
- amplitudes: float32 [2, 16384], P(None, ('grp', 'cuts')), parts along dimension 1
- log_scale: float32 [2], P('grp'), parts along dimension 0
There are 2 independent parts, one for each index of `grp`. A program takes and returns all parts, laid end to end along the dimension named above; an argument that names none is the same for every part. Nothing has to cross between parts.
All inputs are finite; a program needn't handle non-finite values.
Results may differ from a plain program's by a relative error of at most 0.007.
Values sent between devices are 32-bit elements; how exact they have to be, the bound alone decides.
No kernel may reach another device: no remote copies, remote signals or barrier semaphores. Data moves between devices by JAX's collectives and lax.ppermute only.
A program may use at most 128 MiB of HBM per device.

v0:
```python
import jax
import jax.numpy as jnp
from jax import lax
from jax.sharding import PartitionSpec as P


def joined(value, axis, join):
    pieces = lax.all_gather(value, axis)
    head = pieces[0]
    tail = pieces[1:]
    subtotal, _ = lax.scan(lambda subtotal, slab: (join(subtotal, slab), None), head, tail)
    return subtotal


def block_weights(matrices):
    blocks = []
    for value in range(2):
        real_w = matrices[value, 0]
        imag_w = matrices[value, 1]
        upper = jnp.concatenate([real_w, imag_w], axis=1)
        lower = jnp.concatenate([-imag_w, real_w], axis=1)
        blocks.append(jnp.concatenate([upper, lower], axis=0))
    return jnp.concatenate(blocks, axis=1)


def step_product(state, wide, values):
    slices, rows, double = state.shape
    flat = jnp.dot(state.reshape(slices * rows, double), wide, preferred_element_type=jnp.float32)
    flat = flat.reshape(slices, rows, 2 * double)
    picked = values[:, None, None] == 1
    return jnp.where(picked, flat[:, :, double:], flat[:, :, :double])


def add_tables(first, second):
    return first + second


def own_range(values):
    count = values.shape[0] // lax.axis_size("cuts")
    start = lax.axis_index("cuts") * count
    return lax.dynamic_slice_in_dim(values, start, count)


def shards(stem_tensor, branch_tensors, cut_values, bit_rows, bit_cols):
    width = stem_tensor.shape[3]
    state = jnp.concatenate([stem_tensor[0], stem_tensor[1]], axis=2)
    log_scale = jnp.zeros((1,), jnp.float32)
    total_steps = branch_tensors.shape[0]
    for step in range(total_steps):
        product = step_product(state, block_weights(branch_tensors[step]), cut_values[:, step])
        real_part = product[:, :, :width]
        imag_part = product[:, :, width:]
        local_peak = jnp.max(real_part * real_part + imag_part * imag_part)
        peak = jnp.sqrt(lax.pmax(local_peak, "cuts")) + 1e-06
        log_scale = log_scale + jnp.log(peak)
        if step + 1 < total_steps:
            state = (product / peak).astype(jnp.bfloat16)
    summed_slices = jnp.sum(product, axis=0)
    partial_value = jnp.stack([summed_slices[:, :width], summed_slices[:, width:]])
    flat = partial_value.reshape(2, partial_value.shape[1] * width)
    total = joined(flat, "cuts", add_tables)
    position = own_range(bit_rows) * width + own_range(bit_cols)
    amplitudes = total[:, position] / peak
    return (amplitudes, log_scale)


def solution(mesh):
    placed = (
        P(None, ("grp", "cuts"), None, None),
        P(),
        P(("grp", "cuts"), None),
        P("grp"),
        P("grp"),
    )
    return jax.shard_map(
        shards,
        mesh=mesh,
        in_specs=placed,
        out_specs=(P(None, ("grp", "cuts")), P("grp")),
        check_vma=False,
    )
```

profile of v0, /device:TPU:0, one launch (start us, length us, event | category | flops | bytes accessed | tf_op | source)
XLA Modules:
  0.0 113.1 jit_solution(15754800810012895437)
XLA Ops:
  7.2 0.0 all-gather.2.cloned.1.call-start
  7.2 2.7 %slice_bitcast_fusion.1 = (bf16[2,2,512,512]{3,2,1,0:T(8,128)(2,1)S(1)}, bf16[2,2,512,512]{3,2,1,0:T(8,128)(2,1)S(1)}) fusion(bf16[2,2,2,512,512]{4,3,2,1,0:T(8,128)(2,1)} %param.8), kind=kLoop, calls=%fused_computation.35 | loop fusion | bytes 8388608 | tf_op jit(solution)/shard_map/squeeze | solution.py:50
  9.9 0.0 copy-start.1
  9.9 0.0 copy-start
  9.9 0.1 fusion.40
  10.0 0.1 slice_bitcast_fusion.8
  10.1 0.4 copy-done.1
  10.6 0.3 copy-done
  10.9 0.7 fusion
  11.6 0.1 slice_select_fusion.1
  11.8 0.7 fusion.33
  12.4 1.0 slice_bitcast_fusion.4
  13.4 0.1 fusion.42
  13.5 35.6 %pmax.14 = f32[]{:T(128)} all-reduce(f32[]{:T(128)} %fusion.33), channel_id=1, replica_groups=mesh['grp'=2,'cuts'=16] {'cuts'}, use_global_device_ids=true, to_apply=%region_1.2 | all-reduce | flops 1 | bytes 8 | tf_op jit(solution)/shard_map/pmax | solution.py:54
  49.7 1.9 %fusion.15 = f32[4,32,2048]{2,1,0:T(8,128)S(1)} fusion(bf16[512,512]{1,0:T(8,128)(2,1)S(1)} %get-tuple-element.42, bf16[512,512]{1,0:T(8,128)(2,1)S(1)} %get-tuple-element.45, bf16[512,512]{1,0:T(8,128)(2,1)S(1)} %get-tuple-element.41, bf16[512,512]{1,0:T(8,128)(2,1)} %get-tuple-element.43, bf16[512,512]{1,0:T(8,128)(2,1)S(1)} %get-tuple-element.44, ...), kind=kOutput, calls=%fused_computation.19 | convolution fusion | flops 570687488 | bytes 4718596 | tf_op jit(solution)/shard_map/dot_general | solution.py:28
  51.7 0.1 fusion.44
  51.8 0.1 stack.9
  51.9 0.1 stack.10
  52.0 0.8 pad_maximum_fusion
  52.8 0.0 all-gather.2.cloned.1.call-update
  52.8 0.7 fusion.31
  53.5 30.6 %pmax.15 = f32[]{:T(128)} all-reduce(f32[]{:T(128)} %fusion.31), channel_id=1, replica_groups=mesh['grp'=2,'cuts'=16] {'cuts'}, use_global_device_ids=true, to_apply=%region_6.7 | all-reduce | flops 1 | bytes 8 | tf_op jit(solution)/shard_map/pmax | solution.py:54
  84.8 0.8 compare_select_fusion
  85.6 6.3 %all-gather.2.cloned.1.call-done = f32[16,2,16384]{2,1,0:T(2,128)} async-done(((f32[1,2,16384]{2,1,0:T(2,128)}), f32[16,2,16384]{2,1,0:T(2,128)}) %all-gather.2.cloned.1.call-update) | async-done | bytes 2097168 | tf_op jit(solution)/shard_map/all_gather | solution.py:8
  91.9 0.0 slice-start
  91.9 1.1 slice_bitcast_fusion.10
  92.9 0.5 slice-done
  93.5 1.5 %while.10 = (s32[]{:T(128)}, f32[2,16384]{1,0:T(2,128)S(1)}, f32[15,2,16384]{2,1,0:T(2,128)S(1)}, s32[]{:T(128)}) while((s32[]{:T(128)}, f32[2,16384]{1,0:T(2,128)S(1)}, f32[15,2,16384]{2,1,0:T(2,128)S(1)}, s32[]{:T(128)}) %tuple.42), condition=%wide.region_4.5_spmd, body=%wide.region_3.4_spmd.sunk | while | flops 32770 | bytes 393281 | solution.py:11
  93.5 0.1 bitcast_add_fusion.2
  93.6 0.1 bitcast_add_fusion.2
  93.7 0.1 bitcast_add_fusion.2
  93.8 0.1 bitcast_add_fusion.2
  93.9 0.1 bitcast_add_fusion.2
  94.0 0.1 bitcast_add_fusion.2
  94.1 0.1 bitcast_add_fusion.2
  94.2 0.1 bitcast_add_fusion.2
  94.3 0.1 bitcast_add_fusion.2
  94.4 0.1 bitcast_add_fusion.2
  94.5 0.1 bitcast_add_fusion.2
  94.6 0.1 bitcast_add_fusion.2
  94.7 0.1 bitcast_add_fusion.2
  94.8 0.1 bitcast_add_fusion.2
  94.9 0.1 bitcast_add_fusion.2
  95.0 5.0 %copy.9 = f32[2,16384]{0,1:T(8,128)} copy(f32[2,16384]{1,0:T(2,128)S(1)} %get-tuple-element.19) | data formatting | bytes 262144 | tf_op jit(solution)/shard_map/while | solution.py:11
  100.0 4.4 %gather_fusion = f32[512,2]{1,0:T(8,128)S(1)} fusion(f32[2,16384]{0,1:T(8,128)} %copy.9, s32[1024]{0:T(1024)S(1)} %pad_clamp_fusion), kind=kCustom, calls=%fused_computation | custom fusion | bytes 10240 | tf_op jit(solution)/shard_map/gather | solution.py:63
  104.4 0.7 copy.10
  (5 shorter events, 0.1 us)
Async XLA Ops:
  7.2 84.7 %all-gather.2.cloned.1.call-start = ((), (), s32[]{:S(2)}) async-start(), calls=%async_computation | async-start | bytes 2228224 | tf_op jit(solution)/shard_map/all_gather | solution.py:8
  9.9 0.7 copy-start.1
  9.9 1.0 copy-start
  91.9 1.6 %slice-start = ((f32[16,2,16384]{2,1,0:T(2,128)}), f32[15,2,16384]{2,1,0:T(2,128)S(1)}, s32[]{:S(2)}) async-start(f32[16,2,16384]{2,1,0:T(2,128)} %all-gather.2.cloned.1.call-done), calls=%async_computation.1 | async-start | bytes 3932160 | tf_op jit(solution)/shard_map/slice | solution.py:10
Sparse Core Ops, SparseCore 0:
  52.9 38.9 all-gather.1
where the time goes:
time: 113 us
  blocking collectives  66.2 us (59%)
  between operations  16.7 us (15%)
  local copies, waits for them, and re-layouts  16.3 us (14%)
  waiting for transfers between devices  6.27 us (6%)
  other arithmetic  4.58 us (4%)
  matrix products  2.65 us (2%)
    pmax x2, blocking collectives, shards(): peak = jnp.sqrt(lax.pmax(local_peak, 'cuts')) + 1e-06  66.2 us
    all_gather x1, waiting for transfers between devices, joined(): pieces = lax.all_gather(value, axis)  6.25 us
    while x1, local copies, waits for them, and re-layouts, joined(): lax.scan(lambda subtotal, slab: (join(subtotal, slab), None), head, tail)  4.95 us
    gather x1, local copies, waits for them, and re-layouts, shards(): amplitudes = total[:, position] / peak  4.41 us
    squeeze x1, local copies, waits for them, and re-layouts, shards(): branch_tensors[step]  2.68 us
    dot_general x2, matrix products, step_product(): jnp.dot(state.reshape(slices * rows, double), wide, preferred_element_typ...  2.65 us
  transfers between devices with their start and end apart: 1, of which 1 were waited for; matrix products, arithmetic and copies ran while one was open for 1% of the time, Pallas kernels for 0%

commit v1 on v0

v1 whole, which is shorter than its diff:
```python
import functools

import jax
import jax.numpy as jnp
from jax import lax
from jax.experimental import pallas as pl
from jax.experimental.pallas import tpu as pltpu
from jax.sharding import PartitionSpec as P

LANES = 128
TILE = 8


def fold(values, join):
    rows, columns = values.shape
    parts = [
        values[r : r + TILE, c : c + LANES]
        for r in range(0, rows, TILE)
        for c in range(0, columns, LANES)
    ]
    while len(parts) > 1:
        parts = [join(*parts[i : i + 2]) if i + 1 < len(parts) else parts[i] for i in range(0, len(parts), 2)]
    return parts[0]


def contract_kernel(cuts, stem, branch, out, held, weights, wide, stem_sem, branch_sem):
    _, slices, rows, width = held.shape
    steps = weights.shape[0]
    block = slices * rows
    stem_copy = pltpu.make_async_copy(stem, held, stem_sem)
    stem_copy.start()
    copies = {}
    for step in range(steps):
        for part in range(2):
            for value in range(2):
                copy = pltpu.make_async_copy(
                    branch.at[step, value, part],
                    weights.at[step, part, pl.ds(value * width, width)],
                    branch_sem.at[step, part, value],
                )
                copy.start()
                copies[step, part, value] = copy

    def place(step, part, piece, values):
        where = slice(part * block + piece * rows, part * block + (piece + 1) * rows)
        chosen = cuts[piece, step]
        start = pl.multiple_of(chosen * width, width)
        other = pl.multiple_of((1 - chosen) * width, width)
        wide[step, where, pl.ds(start, width)] = values
        wide[step, where, pl.ds(other, width)] = jnp.zeros_like(values)

    def product(step):
        result = []
        for part in range(2):
            for value in range(2):
                copies[step, part, value].wait()
            result.append(jnp.dot(wide[step], weights[step, part], preferred_element_type=jnp.float32))
        by_real, by_imag = result
        return by_real[:block] - by_imag[block:], by_imag[:block] + by_real[block:]

    stem_copy.wait()
    for part in range(2):
        for piece in range(slices):
            place(0, part, piece, held[part, piece])
    real_part, imag_part = product(0)
    for piece in range(slices):
        where = slice(piece * rows, (piece + 1) * rows)
        place(1, 0, piece, real_part[where].astype(jnp.bfloat16))
        place(1, 1, piece, imag_part[where].astype(jnp.bfloat16))
    square = fold(real_part * real_part + imag_part * imag_part, jnp.maximum)
    first = jnp.sqrt(jnp.max(square, axis=(0, 1), keepdims=True))
    scale = first + 1e-06
    inverse = 1.0 / scale
    real_part, imag_part = product(1)
    real_small = real_part * inverse
    imag_small = imag_part * inverse
    square = fold(real_small * real_small + imag_small * imag_small, jnp.maximum)
    second = jnp.sqrt(jnp.max(square, axis=(0, 1), keepdims=True)) * scale
    for part, whole in enumerate((real_part, imag_part)):
        total = whole[:rows]
        for piece in range(1, slices):
            total = total + whole[piece * rows : (piece + 1) * rows]
        for group in range(width // LANES):
            start = (group * 2 + part) * rows
            out[start : start + rows, :] = total[:, group * LANES : (group + 1) * LANES]
    index = lax.broadcasted_iota(jnp.int32, (TILE, LANES), 0)
    out[2 * rows * (width // LANES) :, :] = jnp.where(index == 0, first, second)


def contract(stem, branch, cuts):
    _, slices, rows, width = stem.shape
    steps = branch.shape[0]
    entries = 2 * rows * width // LANES
    return pl.pallas_call(
        contract_kernel,
        out_shape=jax.ShapeDtypeStruct((entries + TILE, LANES), jnp.float32),
        in_specs=[
            pl.BlockSpec(memory_space=pltpu.SMEM),
            pl.BlockSpec(memory_space=pl.ANY),
            pl.BlockSpec(memory_space=pl.ANY),
        ],
        out_specs=pl.BlockSpec(memory_space=pltpu.VMEM),
        scratch_shapes=[
            pltpu.VMEM(stem.shape, jnp.bfloat16),
            pltpu.VMEM((steps, 2, 2 * width, width), jnp.bfloat16),
            pltpu.VMEM((steps, 2 * slices * rows, 2 * width), jnp.bfloat16),
            pltpu.SemaphoreType.DMA,
            pltpu.SemaphoreType.DMA((steps, 2, 2)),
        ],
        cost_estimate=pl.CostEstimate(
            flops=steps * 16 * slices * rows * width * width, bytes_accessed=branch.size * 2, transcendentals=0
        ),
        name="contract",
    )(cuts, stem, branch)


def lookup_kernel(rows, chunks, place, own, got, bit_rows, bit_cols, out):
    entries = own.shape[0] - TILE
    groups = entries // (2 * rows)
    per_chunk = bit_rows.shape[0] // (2 * chunks * 2)
    table = own[:entries, :] + got[:entries, :]
    high = table.astype(jnp.bfloat16)
    low = (table - high.astype(jnp.float32)).astype(jnp.bfloat16)
    left = jnp.concatenate([high, low], axis=1)
    lane = lax.broadcasted_iota(jnp.int32, (LANES, LANES), 0)
    row = lax.broadcasted_iota(jnp.int32, (TILE, LANES), 0)

    def one(chunk, carry):
        first = (place[0] + chunk * place[1]) * per_chunk
        for group in range(per_chunk):
            wanted_col = bit_cols[pl.ds(first + group, 1), :]
            wanted_row = bit_rows[pl.ds(first + group, 1), :]
            hot = jnp.where(lane == (wanted_col & (LANES - 1)), 1.0, 0.0).astype(jnp.bfloat16)
            values = jnp.dot(left, jnp.concatenate([hot, hot], axis=0), preferred_element_type=jnp.float32)
            code = (wanted_col // LANES) * rows + wanted_row
            found = [jnp.zeros((TILE, LANES), jnp.float32) for _ in range(2)]
            for part_group in range(groups):
                for start in range(0, rows, TILE):
                    here = row + (part_group * rows + start) == code
                    for part in range(2):
                        begin = (part_group * 2 + part) * rows + start
                        found[part] = found[part] + jnp.where(here, values[begin : begin + TILE], 0.0)
            for part in range(2):
                out[chunk, pl.ds(2 * group + part, 1), :] = jnp.sum(found[part], axis=0, keepdims=True)
        return carry

    for chunk in range(chunks):
        one(chunk, 0)
    out[chunks] = jnp.maximum(own[entries:, :], got[entries:, :])


def lookup(rows, chunks, place, own, got, bit_rows, bit_cols):
    vmem = pl.BlockSpec(memory_space=pltpu.VMEM)
    return pl.pallas_call(
        functools.partial(lookup_kernel, rows, chunks),
        out_shape=jax.ShapeDtypeStruct((chunks + 1, TILE, LANES), jnp.float32),
        in_specs=[pl.BlockSpec(memory_space=pltpu.SMEM), vmem, vmem, vmem, vmem],
        out_specs=vmem,
        cost_estimate=pl.CostEstimate(flops=chunks * 2 * 512 * 256 * 256, bytes_accessed=1 << 20, transcendentals=0),
        name="lookup",
    )(place, own, got, bit_rows, bit_cols)


def swap(value, bit):
    return lax.ppermute(value, "cuts", [(i, i ^ bit) for i in range(lax.axis_size("cuts"))])


def merge(kept, arrived):
    return jnp.concatenate([kept[:-1] + arrived[:-1], jnp.maximum(kept[-1:], arrived[-1:])])


def exchange(held, bit, radix):
    mine = (lax.axis_index("cuts") // bit) % radix
    share = (held.shape[0] - 1) // radix

    def of(index):
        return jnp.concatenate([lax.dynamic_slice_in_dim(held, index * share, share), held[-1:]])

    arrived = [swap(of(mine ^ other), bit * other) for other in range(radix - 1, 0, -1)]
    result = of(mine)
    for value in arrived:
        result = merge(result, value)
    return result


def shards(stem_tensor, branch_tensors, cut_values, bit_rows, bit_cols):
    rows, width = stem_tensor.shape[2:]
    devices = lax.axis_size("cuts")
    half = devices // 4
    own = contract(stem_tensor, branch_tensors, cut_values)
    got = swap(own, 1)
    me = lax.axis_index("cuts")
    core, side = me % 2, (me // 2) % 2
    row_lines = bit_rows.reshape(-1, LANES)
    col_lines = bit_cols.reshape(-1, LANES)

    def chosen(which):
        place = jnp.stack([2 * which + core, jnp.int32(4)]).astype(jnp.int32)
        return lookup(rows, half, place, own, got, row_lines, col_lines)

    arrived = swap(chosen(1 - side), 2)
    held = merge(chosen(side), arrived)
    bit = 4
    while bit < devices:
        radix = 4 if bit * 4 <= devices else 2
        held = exchange(held, bit, radix)
        bit *= radix
    first = held[1, 0, 0] + 1e-06
    second = held[1, 1, 0] / first + 1e-06
    chunk = held[0].reshape(-1, 2, LANES).transpose(1, 0, 2).reshape(2, -1)
    amplitudes = chunk / first / second
    log_scale = jnp.log(first) + jnp.log(second)
    return amplitudes, log_scale.reshape(1)


def solution(mesh):
    placed = (
        P(None, ("grp", "cuts"), None, None),
        P(),
        P(("grp", "cuts"), None),
        P("grp"),
        P("grp"),
    )
    return jax.shard_map(
        shards,
        mesh=mesh,
        in_specs=placed,
        out_specs=(P(None, ("grp", "cuts")), P("grp")),
        check_vma=False,
    )
```

time: 113 us -> 31.2 us (0.28)
  blocking collectives: 66.2 us -> 0 us
  local copies, waits for them, and re-layouts: 16.3 us -> 2.51 us
  between operations: 16.7 us -> 3.18 us
  Pallas kernels: 0 us -> 10.1 us
  starting transfers between devices: 0.04 us -> 7.9 us
  matrix products: 2.65 us -> 0 us
  waiting for transfers between devices: 6.27 us -> 3.91 us
  other arithmetic: 4.58 us -> 3.24 us
    pmax x2 -> x0, blocking collectives: 66.2 us -> none  [shards(): peak = jnp.sqrt(lax.pmax(local_peak, 'cuts')) + 1e-06]
    pallas_call x0 -> x3, Pallas kernels: none -> 10.1 us  [the longest x1 5.5 us: contract(): pl.pallas_call(contract_kernel, out_shape=jax.ShapeDtypeStruct((entries +...]
    ppermute x0 -> x5, starting transfers between devices: none -> 7.9 us  [swap(): lax.ppermute(value, 'cuts', [(i, i ^ bit) for i in range(lax.axis_size('c...]
    all_gather x1 -> x0, waiting for transfers between devices: 6.25 us -> none  [joined(): pieces = lax.all_gather(value, axis)]
    while x1 -> x0, local copies, waits for them, and re-layouts: 4.95 us -> none  [joined(): lax.scan(lambda subtotal, slab: (join(subtotal, slab), None), head, tail)]
    squeeze x4 -> x0, local copies, waits for them, and re-layouts: 4.83 us -> none  [the longest x1 2.68 us: shards(): branch_tensors[step]]
    gather x1 -> x0, local copies, waits for them, and re-layouts: 4.41 us -> none  [shards(): amplitudes = total[:, position] / peak]
    ppermute x0 -> x5, waiting for transfers between devices: none -> 3.91 us  [swap(): lax.ppermute(value, 'cuts', [(i, i ^ bit) for i in range(lax.axis_size('c...]
  transfers between devices with their start and end apart: 1 -> 5, of which waited for: 1 -> 2; matrix products, arithmetic and copies ran while one was open for 1% -> 4% of each run, Pallas kernels for 0% -> 7%
where the time goes in v1:
time: 31.2 us; the launch traced here: 30.8 us
  Pallas kernels  10.1 us (32%)
  starting transfers between devices  7.9 us (25%)
  waiting for transfers between devices  3.91 us (13%)
  other arithmetic  3.24 us (10%)
  between operations  3.18 us (10%)
  local copies, waits for them, and re-layouts  2.51 us (8%)
    ppermute x5, starting transfers between devices, swap(): lax.ppermute(value, 'cuts', [(i, i ^ bit) for i in range(lax.axis_size('c...  7.9 us
    pallas_call x1, Pallas kernels, contract(): pl.pallas_call(contract_kernel, out_shape=jax.ShapeDtypeStruct((entries +...  5.5 us
    pallas_call x2, Pallas kernels, lookup(): pl.pallas_call(functools.partial(lookup_kernel, rows, chunks), out_shape=...  4.59 us
    ppermute x5, waiting for transfers between devices, swap(): lax.ppermute(value, 'cuts', [(i, i ^ bit) for i in range(lax.axis_size('c...  3.91 us
    unnamed x3, local copies, waits for them, and re-layouts  1.99 us
    another operation x2, other arithmetic, chosen(): place = jnp.stack([2 * which + core, jnp.int32(4)]).astype(jnp.int32)  1.2 us
    add x1, other arithmetic, merge(): kept[:-1] + arrived[:-1]  0.72 us
    max x2, other arithmetic, merge(): jnp.maximum(kept[-1:], arrived[-1:])  0.69 us
  transfers between devices with their start and end apart: 5, of which 2 were waited for; matrix products, arithmetic and copies ran while one was open for 4% of the time, Pallas kernels for 7%

profile of v1, /device:TPU:0, one launch (start us, length us, event | category | flops | bytes accessed | tf_op | source)
XLA Modules:
  0.0 30.8 jit_solution(1338039601648267226)
XLA Ops:
  0.6 1.3 %copy.7.cuts = s32[4,2]{1,0:T(4,128)} copy(s32[4,2]{0,1:T(2,128)} %param.7) | data formatting | bytes 64 | tf_op args[2]
  2.0 5.5 %contract.1.own = f32[264,128]{1,0:T(8,128)} custom-call(s32[4,2]{1,0:T(4,128)} %copy.7.cuts, bf16[2,4,32,512]{3,2,1,0:T(8,128)(2,1)} %stem.1, bf16[2,2,2,512,512]{4,3,2,1,0:T(8,128)(2,1)} %branch.1), custom_call_target="tpu_custom_call" | custom-call | flops 1073741824 | bytes 4194304 | tf_op jit(solution)/shard_map/contract/pallas_call | solution.py:94
  7.5 0.6 %collective-permute-start = (f32[264,128]{1,0:T(8,128)}, f32[264,128]{1,0:T(8,128)S(1)}, u32[]{:S(2)}, u32[]{:S(2)}) collective-permute-start(f32[264,128]{1,0:T(8,128)} %contract.1.own), channel_id=1, source_target_pairs={{0,1},{1,0},{2,3},{3,2},{4,5},{5,4},{6,7},{7,6},{8,9},{9,8},{10,11... | collective-permute-start | bytes 405512 | tf_op jit(solution)/shard_map/ppermute | solution.py:165
  8.0 0.6 %pad_add_fusion.1.place = s32[2]{0:T(128)} fusion(s32[1]{0:T(128)} %constant.55.clone.1, s32[1]{0:T(128)} %bitcast), kind=kLoop, calls=%fused_computation.25 | loop fusion | flops 2 | bytes 16 | tf_op jit(solution)/shard_map/stack | solution.py:198
  8.6 0.6 %pad_add_fusion.place = s32[2]{0:T(128)} fusion(s32[1]{0:T(128)} %constant.55.clone.1, s32[1]{0:T(128)} %bitcast.3), kind=kLoop, calls=%fused_computation.24 | loop fusion | flops 2 | bytes 16 | tf_op jit(solution)/shard_map/stack | solution.py:198
  9.2 0.0 collective-permute-done.got
  9.2 0.0 copy-start
  9.2 0.7 %copy-done = f32[264,128]{1,0:T(8,128)} copy-done((f32[264,128]{1,0:T(8,128)}, f32[264,128]{1,0:T(8,128)S(1)}, u32[]{:S(2)}) %copy-start) | copy-done | bytes 135192
  9.9 2.3 %lookup.3 = f32[5,8,128]{2,1,0:T(8,128)} custom-call(s32[2]{0:T(128)} %pad_add_fusion.place, f32[264,128]{1,0:T(8,128)} %contract.1.own, f32[264,128]{1,0:T(8,128)} %copy-done, s32[64,128]{1,0:T(8,128)} %bitcast.13, s32[64,128]{1,0:T(8,128)} %bitcast.15), custom_call_target="tpu_custom_call" | custom-call | flops 268435456 | bytes 1048576 | tf_op jit(solution)/shard_map/lookup/pallas_call | solution.py:154
  12.2 2.9 %collective-permute-start.1 = (f32[5,8,128]{2,1,0:T(8,128)}, f32[5,8,128]{2,1,0:T(8,128)S(1)}, u32[]{:S(2)}, u32[]{:S(2)}) collective-permute-start(f32[5,8,128]{2,1,0:T(8,128)} %lookup.3), channel_id=1, source_target_pairs={{0,2},{1,3},{2,0},{3,1},{4,6},{5,7},{6,4},{7,5},{8,10},{9,11},{10,... | collective-permute-start | bytes 61448 | tf_op jit(solution)/shard_map/ppermute | solution.py:165
  15.0 2.3 %lookup.2 = f32[5,8,128]{2,1,0:T(8,128)} custom-call(s32[2]{0:T(128)} %pad_add_fusion.1.place, f32[264,128]{1,0:T(8,128)} %contract.1.own, f32[264,128]{1,0:T(8,128)} %copy-done, s32[64,128]{1,0:T(8,128)} %bitcast.14, s32[64,128]{1,0:T(8,128)} %bitcast.16), custom_call_target="tpu_custom_call" | custom-call | flops 268435456 | bytes 1048576 | tf_op jit(solution)/shard_map/lookup/pallas_call | solution.py:154
  17.3 0.0 collective-permute-done.1
  17.3 0.7 %slice_maximum_fusion.3 = f32[1,8,128]{2,1,0:T(8,128)S(1)} fusion(f32[5,8,128]{2,1,0:T(8,128)S(1)} %collective-permute-done.1, f32[5,8,128]{2,1,0:T(8,128)} %lookup.2), kind=kLoop, calls=%fused_computation.23 | loop fusion | flops 1024 | bytes 12288 | tf_op jit(solution)/shard_map/max | solution.py:169
  18.0 0.7 %slice_add_fusion = f32[4,8,128]{2,1,0:T(8,128)S(1)} fusion(f32[5,8,128]{2,1,0:T(8,128)S(1)} %collective-permute-done.1, f32[5,8,128]{2,1,0:T(8,128)} %lookup.2), kind=kLoop, calls=%fused_computation.8 | loop fusion | flops 4096 | bytes 49152 | tf_op jit(solution)/shard_map/add | solution.py:169
  18.8 3.8 %collective-permute-start.2 = (f32[2,8,128]{2,1,0:T(8,128)S(1)}, f32[2,8,128]{2,1,0:T(8,128)S(1)}, u32[]{:S(2)}, u32[]{:S(2)}) collective-permute-start(f32[2,8,128]{2,1,0:T(8,128)S(1)} %get-tuple-element.7), channel_id=1, source_target_pairs={{0,12},{1,13},{2,14},{3,15},{4,8},{5,9},{6,10},{7,11},{8,4},{9,5},... | collective-permute-start | bytes 24584 | tf_op jit(solution)/shard_map/ppermute | solution.py:165
  22.6 0.0 collective-permute-start.3
  22.6 0.6 %collective-permute-start.4 = (f32[2,8,128]{2,1,0:T(8,128)S(1)}, f32[2,8,128]{2,1,0:T(8,128)S(1)}, u32[]{:S(2)}, u32[]{:S(2)}) collective-permute-start(f32[2,8,128]{2,1,0:T(8,128)S(1)} %get-tuple-element.9), channel_id=1, source_target_pairs={{0,4},{1,5},{2,6},{3,7},{4,0},{5,1},{6,2},{7,3},{8,12},{9,13},{10,... | collective-permute-start | bytes 24584 | tf_op jit(solution)/shard_map/ppermute | solution.py:165
  23.3 1.0 %collective-permute-done.2 = f32[2,8,128]{2,1,0:T(8,128)S(1)} collective-permute-done((f32[2,8,128]{2,1,0:T(8,128)S(1)}, f32[2,8,128]{2,1,0:T(8,128)S(1)}, u32[]{:S(2)}, u32[]{:S(2)}) %collective-permute-start.2) | collective-permute-done | bytes 8224 | tf_op jit(solution)/shard_map/ppermute | solution.py:165
  24.3 2.9 %collective-permute-done.3 = f32[2,8,128]{2,1,0:T(8,128)S(1)} collective-permute-done((f32[2,8,128]{2,1,0:T(8,128)S(1)}, f32[2,8,128]{2,1,0:T(8,128)S(1)}, u32[]{:S(2)}, u32[]{:S(2)}) %collective-permute-start.3) | collective-permute-done | bytes 8224 | tf_op jit(solution)/shard_map/ppermute | solution.py:165
  27.2 0.0 collective-permute-done.4
  27.2 0.5 %fusion.8 = (f32[1,1,1]{2,1,0:T(1,128)}, f32[1,1,1]{2,1,0:T(1,128)}) fusion(f32[1,8,128]{2,1,0:T(8,128)S(1)} %slice_maximum_fusion), kind=kLoop, calls=%fused_computation.26 | loop fusion | bytes 16 | tf_op jit(solution)/shard_map/slice | solution.py:209
  29.1 0.6 %fusion.5 = f32[1,8,128]{2,1,0:T(8,128)} fusion(s32[]{:T(128)S(6)} %select_n.39, f32[4,8,128]{2,1,0:T(8,128)S(1)} %slice_add_fusion, f32[1,8,128]{2,1,0:T(8,128)S(1)} %slice_maximum_fusion.3, f32[2,8,128]{2,1,0:T(8,128)S(1)} %collective-permute-done.4, f32[2,8,128]{2,1,0:T(8,128)S(1)} %collective-permute-done.3, f32[2,8,128]{2,1,0:T(8,128)S(1)} %collective-permute-done.2, ...), kind=kLoop, calls=%fused_computation.17 | loop fusion | flops 5120 | bytes 36872 | tf_op jit(solution)/shard_map/div | solution.py:211
  (3 shorter events, 0.0 us)
Async XLA Ops:
  7.5 1.8 %collective-permute-start = (f32[264,128]{1,0:T(8,128)}, f32[264,128]{1,0:T(8,128)S(1)}, u32[]{:S(2)}, u32[]{:S(2)}) collective-permute-start(f32[264,128]{1,0:T(8,128)} %contract.1.own), channel_id=1, source_target_pairs={{0,1},{1,0},{2,3},{3,2},{4,5},{5,4},{6,7},{7,6},{8,9},{9,8},{10,11... | collective-permute-start | bytes 405512 | tf_op jit(solution)/shard_map/ppermute | solution.py:165
  9.2 0.7 %copy-start = (f32[264,128]{1,0:T(8,128)}, f32[264,128]{1,0:T(8,128)S(1)}, u32[]{:S(2)}) copy-start(f32[264,128]{1,0:T(8,128)S(1)} %collective-permute-done.got) | copy-start | bytes 405508
  12.2 5.2 %collective-permute-start.1 = (f32[5,8,128]{2,1,0:T(8,128)}, f32[5,8,128]{2,1,0:T(8,128)S(1)}, u32[]{:S(2)}, u32[]{:S(2)}) collective-permute-start(f32[5,8,128]{2,1,0:T(8,128)} %lookup.3), channel_id=1, source_target_pairs={{0,2},{1,3},{2,0},{3,1},{4,6},{5,7},{6,4},{7,5},{8,10},{9,11},{10,... | collective-permute-start | bytes 61448 | tf_op jit(solution)/shard_map/ppermute | solution.py:165
  18.8 5.5 %collective-permute-start.2 = (f32[2,8,128]{2,1,0:T(8,128)S(1)}, f32[2,8,128]{2,1,0:T(8,128)S(1)}, u32[]{:S(2)}, u32[]{:S(2)}) collective-permute-start(f32[2,8,128]{2,1,0:T(8,128)S(1)} %get-tuple-element.7), channel_id=1, source_target_pairs={{0,12},{1,13},{2,14},{3,15},{4,8},{5,9},{6,10},{7,11},{8,4},{9,5},... | collective-permute-start | bytes 24584 | tf_op jit(solution)/shard_map/ppermute | solution.py:165
  22.6 4.5 %collective-permute-start.3 = (f32[2,8,128]{2,1,0:T(8,128)S(1)}, f32[2,8,128]{2,1,0:T(8,128)S(1)}, u32[]{:S(2)}, u32[]{:S(2)}) collective-permute-start(f32[2,8,128]{2,1,0:T(8,128)S(1)} %get-tuple-element.8), channel_id=1, source_target_pairs={{0,8},{1,9},{2,10},{3,11},{4,12},{5,13},{6,14},{7,15},{8,0},{9,1},... | collective-permute-start | bytes 24584 | tf_op jit(solution)/shard_map/ppermute | solution.py:165
  22.6 4.5 %collective-permute-start.4 = (f32[2,8,128]{2,1,0:T(8,128)S(1)}, f32[2,8,128]{2,1,0:T(8,128)S(1)}, u32[]{:S(2)}, u32[]{:S(2)}) collective-permute-start(f32[2,8,128]{2,1,0:T(8,128)S(1)} %get-tuple-element.9), channel_id=1, source_target_pairs={{0,4},{1,5},{2,6},{3,7},{4,0},{5,1},{6,2},{7,3},{8,12},{9,13},{10,... | collective-permute-start | bytes 24584 | tf_op jit(solution)/shard_map/ppermute | solution.py:165

commit v2 on v1

v2 whole, which is shorter than its diff:
```python
import functools

import jax
import jax.numpy as jnp
from jax import lax
from jax.experimental import pallas as pl
from jax.experimental.pallas import tpu as pltpu
from jax.sharding import PartitionSpec as P

LANES = 128
TILE = 8


def fold(values, join):
    rows, columns = values.shape
    parts = [
        values[r : r + TILE, c : c + LANES]
        for r in range(0, rows, TILE)
        for c in range(0, columns, LANES)
    ]
    while len(parts) > 1:
        parts = [join(*parts[i : i + 2]) if i + 1 < len(parts) else parts[i] for i in range(0, len(parts), 2)]
    return parts[0]


def contract_kernel(cuts_in, stem, branch, rows_in, cols_in, out, lane_of, line_of, cuts, held, weights, wide, wanted, sems, branch_sem):
    _, slices, rows, width = held.shape
    steps = weights.shape[0]
    block = slices * rows
    cuts_copy = pltpu.make_async_copy(cuts_in, cuts, sems.at[0])
    stem_copy = pltpu.make_async_copy(stem, held, sems.at[1])
    cuts_copy.start()
    stem_copy.start()
    copies = {}
    for step in range(steps):
        for part in range(2):
            for value in range(2):
                copy = pltpu.make_async_copy(
                    branch.at[step, value, part],
                    weights.at[step, part, pl.ds(value * width, width)],
                    branch_sem.at[step, part, value],
                )
                copy.start()
                copies[step, part, value] = copy
    rows_copy = pltpu.make_async_copy(rows_in, wanted.at[0], sems.at[2])
    cols_copy = pltpu.make_async_copy(cols_in, wanted.at[1], sems.at[3])
    rows_copy.start()
    cols_copy.start()
    cuts_copy.wait()
    stem_copy.wait()

    def place(step, part, piece, values):
        where = slice(part * block + piece * rows, part * block + (piece + 1) * rows)
        chosen = cuts[step, piece]
        start = pl.multiple_of(chosen * width, width)
        other = pl.multiple_of((1 - chosen) * width, width)
        wide[step, where, pl.ds(start, width)] = values
        wide[step, where, pl.ds(other, width)] = jnp.zeros_like(values)

    def product(step):
        result = []
        for part in range(2):
            for value in range(2):
                copies[step, part, value].wait()
            result.append(jnp.dot(wide[step], weights[step, part], preferred_element_type=jnp.float32))
        by_real, by_imag = result
        return by_real[:block] - by_imag[block:], by_imag[:block] + by_real[block:]

    for part in range(2):
        for piece in range(slices):
            place(0, part, piece, held[part, piece])
    real_part, imag_part = product(0)
    for piece in range(slices):
        where = slice(piece * rows, (piece + 1) * rows)
        place(1, 0, piece, real_part[where].astype(jnp.bfloat16))
        place(1, 1, piece, imag_part[where].astype(jnp.bfloat16))
    square = fold(real_part * real_part + imag_part * imag_part, jnp.maximum)
    first = jnp.sqrt(jnp.max(square, axis=(0, 1), keepdims=True))
    scale = first + 1e-06
    inverse = 1.0 / scale
    rows_copy.wait()
    cols_copy.wait()
    columns = wanted[1]
    lane_of[...] = columns % LANES
    line_of[...] = columns // LANES * rows + wanted[0]
    real_part, imag_part = product(1)
    real_small = real_part * inverse
    imag_small = imag_part * inverse
    square = fold(real_small * real_small + imag_small * imag_small, jnp.maximum)
    second = jnp.sqrt(jnp.max(square, axis=(0, 1), keepdims=True)) * scale
    for part, whole in enumerate((real_part, imag_part)):
        total = whole[:rows]
        for piece in range(1, slices):
            total = total + whole[piece * rows : (piece + 1) * rows]
        for group in range(width // LANES):
            start = (group * 2 + part) * rows
            out[start : start + rows, :] = total[:, group * LANES : (group + 1) * LANES]
    index = lax.broadcasted_iota(jnp.int32, (TILE, LANES), 0)
    out[2 * rows * (width // LANES) :, :] = jnp.where(index == 0, first, second)


def in_hbm(value):
    return pltpu.with_memory_space_constraint(value, pltpu.HBM)


def in_vmem(value):
    return pltpu.with_memory_space_constraint(value, pltpu.VMEM)


def contract(stem, branch, cuts, bit_rows, bit_cols):
    _, slices, rows, width = stem.shape
    steps = branch.shape[0]
    entries = 2 * rows * width // LANES
    return pl.pallas_call(
        contract_kernel,
        out_shape=(
            pltpu.VMEM((entries + TILE, LANES), jnp.float32),
            pltpu.VMEM(bit_rows.shape, jnp.int32),
            pltpu.VMEM(bit_rows.shape, jnp.int32),
        ),
        in_specs=[pl.BlockSpec(memory_space=pl.ANY)] * 5,
        out_specs=[pl.BlockSpec(memory_space=pltpu.VMEM)] * 3,
        scratch_shapes=[
            pltpu.SMEM((steps, slices), jnp.int32),
            pltpu.VMEM(stem.shape, jnp.bfloat16),
            pltpu.VMEM((steps, 2, 2 * width, width), jnp.bfloat16),
            pltpu.VMEM((steps, 2 * slices * rows, 2 * width), jnp.bfloat16),
            pltpu.VMEM((2, *bit_rows.shape), jnp.int32),
            pltpu.SemaphoreType.DMA((4,)),
            pltpu.SemaphoreType.DMA((steps, 2, 2)),
        ],
        compiler_params=pltpu.CompilerParams(vmem_limit_bytes=32 << 20),
        cost_estimate=pl.CostEstimate(
            flops=steps * 16 * slices * rows * width * width, bytes_accessed=branch.size * 2, transcendentals=0
        ),
        name="contract",
    )(in_hbm(cuts.T), in_hbm(stem), in_hbm(branch), in_hbm(bit_rows), in_hbm(bit_cols))


def lookup_kernel(rows, chunks, other, own, got, lane_of, line_of, out):
    entries = own.shape[0] - TILE
    groups = entries // (2 * rows)
    per_chunk = lane_of.shape[0] // (2 * chunks * 2)
    me = lax.axis_index("cuts")
    side = (me // 2) % 2
    which = 2 * (1 - side if other else side) + me % 2
    table = own[:entries, :] + got[:entries, :]
    high = table.astype(jnp.bfloat16)
    low = (table - high.astype(jnp.float32)).astype(jnp.bfloat16)
    left = jnp.concatenate([high, low], axis=1)
    lane = lax.broadcasted_iota(jnp.int32, (LANES, LANES), 0)
    row = lax.broadcasted_iota(jnp.int32, (TILE, LANES), 0)

    def hot(line):
        return jnp.where(lane == lane_of[pl.ds(line, 1), :], 1.0, 0.0).astype(jnp.bfloat16)

    for chunk in range(chunks):
        first = (which + 4 * chunk) * per_chunk
        for pair in range(0, per_chunk, 2):
            right = jnp.concatenate([hot(first + pair), hot(first + pair + 1)], axis=1)
            both = jnp.dot(left, jnp.concatenate([right, right], axis=0), preferred_element_type=jnp.float32)
            for group in range(2):
                values = both[:, group * LANES : (group + 1) * LANES]
                wanted = line_of[pl.ds(first + pair + group, 1), :]
                found = [jnp.zeros((TILE, LANES), jnp.float32) for _ in range(2)]
                for part_group in range(groups):
                    for start in range(0, rows, TILE):
                        here = row + (part_group * rows + start) == wanted
                        for part in range(2):
                            begin = (part_group * 2 + part) * rows + start
                            found[part] = found[part] + jnp.where(here, values[begin : begin + TILE], 0.0)
                for part in range(2):
                    out[chunk, pl.ds(2 * (pair + group) + part, 1), :] = jnp.sum(found[part], axis=0, keepdims=True)
    out[chunks] = jnp.maximum(own[entries:, :], got[entries:, :])


def lookup(rows, chunks, other, *operands):
    vmem = pl.BlockSpec(memory_space=pltpu.VMEM)
    return pl.pallas_call(
        functools.partial(lookup_kernel, rows, chunks, other),
        out_shape=pltpu.VMEM((chunks + 1, TILE, LANES), jnp.float32),
        in_specs=[vmem] * 4,
        out_specs=vmem,
        compiler_params=pltpu.CompilerParams(vmem_limit_bytes=16 << 20),
        cost_estimate=pl.CostEstimate(flops=chunks * 2 * 512 * 256 * 256, bytes_accessed=1 << 20, transcendentals=0),
        name="lookup",
    )(*map(in_vmem, operands))


def finish_kernel(own, *rest):
    *arrived, amplitudes, log_scale = rest
    total = own[0]
    peaks = own[1]
    for value in arrived:
        total = total + value[0]
        peaks = jnp.maximum(peaks, value[1])
    first = peaks[0:1] + 1e-06
    second = peaks[1:2] / first + 1e-06
    total = total / first / second
    for group in range(TILE // 2):
        amplitudes[:, group * LANES : (group + 1) * LANES] = total[2 * group : 2 * group + 2]
    log_scale[...] = (jnp.log(first) + jnp.log(second))[:, :1]


def finish(*held):
    vmem = pl.BlockSpec(memory_space=pltpu.VMEM)
    amplitudes, log_scale = pl.pallas_call(
        finish_kernel,
        out_shape=(
            jax.ShapeDtypeStruct((2, TILE // 2 * LANES), jnp.float32),
            jax.ShapeDtypeStruct((1, 1), jnp.float32),
        ),
        in_specs=[vmem] * len(held),
        out_specs=[vmem] * 2,
        compiler_params=pltpu.CompilerParams(vmem_limit_bytes=1 << 20),
        name="finish",
    )(*map(in_vmem, held))
    return amplitudes, log_scale.reshape(1)


def swap(value, bit):
    return lax.ppermute(value, "cuts", [(i, i ^ bit) for i in range(lax.axis_size("cuts"))])


def merge(kept, arrived):
    return jnp.concatenate([kept[:-1] + arrived[:-1], jnp.maximum(kept[-1:], arrived[-1:])])


def exchange(held, bit, radix):
    mine = (lax.axis_index("cuts") // bit) % radix
    share = (held.shape[0] - 1) // radix

    def of(index):
        return jnp.concatenate([lax.dynamic_slice_in_dim(held, index * share, share), held[-1:]])

    arrived = [swap(of(mine ^ other), bit * other) for other in range(radix - 1, 0, -1)]
    return [of(mine), *arrived]


def shards(stem_tensor, branch_tensors, cut_values, bit_rows, bit_cols):
    rows, width = stem_tensor.shape[2:]
    devices = lax.axis_size("cuts")
    half = devices // 4
    own, lane_of, line_of = contract(
        stem_tensor, branch_tensors, cut_values, bit_rows.reshape(-1, LANES), bit_cols.reshape(-1, LANES)
    )
    got = swap(own, 1)
    arrived = swap(lookup(rows, half, True, own, got, lane_of, line_of), 2)
    pieces = [lookup(rows, half, False, own, got, lane_of, line_of), arrived]
    bit = 4
    while bit < devices:
        radix = 4 if bit * 4 <= devices else 2
        pieces = exchange(functools.reduce(merge, pieces), bit, radix)
        bit *= radix
    return finish(*pieces)


def solution(mesh):
    placed = (
        P(None, ("grp", "cuts"), None, None),
        P(),
        P(("grp", "cuts"), None),
        P("grp"),
        P("grp"),
    )
    return jax.shard_map(
        shards,
        mesh=mesh,
        in_specs=placed,
        out_specs=(P(None, ("grp", "cuts")), P("grp")),
        check_vma=False,
    )
```

time: 31.2 us -> 21.3 us (0.68)
  Pallas kernels: 10.1 us -> 5.58 us
  other arithmetic: 3.24 us -> 0.05 us
  waiting for transfers between devices: 3.91 us -> 6.64 us
  local copies, waits for them, and re-layouts: 2.51 us -> 0 us
  between operations: 3.18 us -> 0.68 us
  starting transfers between devices: 7.9 us -> 8.25 us
    pallas_call x3 -> x4, Pallas kernels: 10.1 us -> 5.58 us  [the longest x1 3.91 us: contract(): pl.pallas_call(contract_kernel, out_shape=(pltpu.VMEM((entries + TILE, LA...]
    ppermute x5, waiting for transfers between devices: 3.91 us -> 6.64 us  [swap(): lax.ppermute(value, 'cuts', [(i, i ^ bit) for i in range(lax.axis_size('c...]
    unnamed x3 -> x0, local copies, waits for them, and re-layouts: 1.99 us -> none
    another operation x2 -> x0, other arithmetic: 1.2 us -> none  [chosen(): place = jnp.stack([2 * which + core, jnp.int32(4)]).astype(jnp.int32)]
    add x1, other arithmetic: 0.72 us -> 0.01 us  [merge(): kept[:-1] + arrived[:-1]]
    max x2 -> x1, other arithmetic: 0.69 us -> 0.01 us  [merge(): jnp.maximum(kept[-1:], arrived[-1:])]
    div x1 -> x0, other arithmetic: 0.61 us -> none  [shards(): amplitudes = chunk / first / second]
    slice x1 -> x0, local copies, waits for them, and re-layouts: 0.52 us -> none  [shards(): second = held[1, 1, 0] / first + 1e-06]
  transfers between devices with their start and end apart: 5 -> 5, of which waited for: 2 -> 4; matrix products, arithmetic and copies ran while one was open for 4% -> 0% of each run, Pallas kernels for 7% -> 2%
where the time goes in v2:
time: 21.3 us; the launch traced here: 21.2 us
  starting transfers between devices  8.25 us (39%)
  waiting for transfers between devices  6.64 us (31%)
  Pallas kernels  5.58 us (26%)
  between operations  0.68 us (3%)
    ppermute x5, starting transfers between devices, swap(): lax.ppermute(value, 'cuts', [(i, i ^ bit) for i in range(lax.axis_size('c...  8.25 us
    ppermute x5, waiting for transfers between devices, swap(): lax.ppermute(value, 'cuts', [(i, i ^ bit) for i in range(lax.axis_size('c...  6.64 us
    pallas_call x1, Pallas kernels, contract(): pl.pallas_call(contract_kernel, out_shape=(pltpu.VMEM((entries + TILE, LA...  3.91 us
    pallas_call x2, Pallas kernels, lookup(): pl.pallas_call(functools.partial(lookup_kernel, rows, chunks, other), out...  1.05 us
    pallas_call x1, Pallas kernels, finish(): pl.pallas_call(finish_kernel, out_shape=(jax.ShapeDtypeStruct((2, TILE //...  0.62 us
  transfers between devices with their start and end apart: 5, of which 4 were waited for; matrix products, arithmetic and copies ran while one was open for 0% of the time, Pallas kernels for 2%

profile of v2, /device:TPU:0, one launch (start us, length us, event | category | flops | bytes accessed | tf_op | source)
XLA Modules:
  0.0 21.2 jit_solution(5061760761068727997)
XLA Ops:
  0.6 3.9 %contract.1 = (f32[264,128]{1,0:T(8,128)S(1)}, s32[64,128]{1,0:T(8,128)S(1)}, s32[64,128]{1,0:T(8,128)S(1)}) custom-call(s32[2,4]{1,0:T(2,128)} %bitcast.6, bf16[2,4,32,512]{3,2,1,0:T(8,128)(2,1)} %stem.1, bf16[2,2,2,512,512]{4,3,2,1,0:T(8,128)(2,1)} %branch.1, s32[64,128]{1,0:T(8,128)} %bitcast.4, s32[64,128]{1,0:T(8,128)} %bitcast.5), custom_call_target="tpu_custom_call" | custom-call | flops 1073741824 | bytes 4194304 | tf_op jit(solution)/shard_map/contract/pallas_call | solution.py:114
  4.5 0.6 %collective-permute-start = (f32[264,128]{1,0:T(8,128)S(1)}, f32[264,128]{1,0:T(8,128)S(1)}, u32[]{:S(2)}, u32[]{:S(2)}) collective-permute-start(f32[264,128]{1,0:T(8,128)S(1)} %get-tuple-element.7.own), channel_id=1, source_target_pairs={{0,1},{1,0},{2,3},{3,2},{4,5},{5,4},{6,7},{7,6},{8,9},{9,8},{10,11... | collective-permute-start | bytes 405512 | tf_op jit(solution)/shard_map/ppermute | solution.py:222
  5.1 1.0 %collective-permute-done.got = f32[264,128]{1,0:T(8,128)S(1)} collective-permute-done((f32[264,128]{1,0:T(8,128)S(1)}, f32[264,128]{1,0:T(8,128)S(1)}, u32[]{:S(2)}, u32[]{:S(2)}) %collective-permute-start) | collective-permute-done | bytes 135200 | tf_op jit(solution)/shard_map/ppermute | solution.py:222
  6.1 0.5 %lookup.3 = f32[5,8,128]{2,1,0:T(8,128)S(1)} custom-call(f32[264,128]{1,0:T(8,128)S(1)} %get-tuple-element.7.own, f32[264,128]{1,0:T(8,128)S(1)} %collective-permute-done.got, s32[64,128]{1,0:T(8,128)S(1)} %get-tuple-element.8.lane_of, s32[64,128]{1,0:T(8,128)S(1)} %get-tuple-element.9.line_of), custom_call_target="tpu_custom_call" | custom-call | flops 268435456 | bytes 1048576 | tf_op jit(solution)/shard_map/lookup/pallas_call | solution.py:179
  6.6 2.9 %collective-permute-start.1 = (f32[5,8,128]{2,1,0:T(8,128)S(1)}, f32[5,8,128]{2,1,0:T(8,128)S(1)}, u32[]{:S(2)}, u32[]{:S(2)}) collective-permute-start(f32[5,8,128]{2,1,0:T(8,128)S(1)} %lookup.3), channel_id=1, source_target_pairs={{0,2},{1,3},{2,0},{3,1},{4,6},{5,7},{6,4},{7,5},{8,10},{9,11},{10,... | collective-permute-start | bytes 61448 | tf_op jit(solution)/shard_map/ppermute | solution.py:222
  9.6 0.5 %lookup.2 = f32[5,8,128]{2,1,0:T(8,128)S(1)} custom-call(f32[264,128]{1,0:T(8,128)S(1)} %get-tuple-element.7.own, f32[264,128]{1,0:T(8,128)S(1)} %collective-permute-done.got, s32[64,128]{1,0:T(8,128)S(1)} %get-tuple-element.8.lane_of, s32[64,128]{1,0:T(8,128)S(1)} %get-tuple-element.9.line_of), custom_call_target="tpu_custom_call" | custom-call | flops 268435456 | bytes 1048576 | tf_op jit(solution)/shard_map/lookup/pallas_call | solution.py:179
  10.1 1.2 %collective-permute-done.1 = f32[5,8,128]{2,1,0:T(8,128)S(1)} collective-permute-done((f32[5,8,128]{2,1,0:T(8,128)S(1)}, f32[5,8,128]{2,1,0:T(8,128)S(1)}, u32[]{:S(2)}, u32[]{:S(2)}) %collective-permute-start.1) | collective-permute-done | bytes 20512 | tf_op jit(solution)/shard_map/ppermute | solution.py:222
  11.4 2.2 %collective-permute-start.4 = (f32[2,8,128]{2,1,0:T(8,128)S(1)}, f32[2,8,128]{2,1,0:T(8,128)S(1)}, u32[]{:S(2)}, u32[]{:S(2)}) collective-permute-start(f32[2,8,128]{2,1,0:T(8,128)S(1)} %get-tuple-element.16), channel_id=1, source_target_pairs={{0,4},{1,5},{2,6},{3,7},{4,0},{5,1},{6,2},{7,3},{8,12},{9,13},{10,... | collective-permute-start | bytes 24584 | tf_op jit(solution)/shard_map/ppermute | solution.py:222
  13.5 2.5 %collective-permute-start.2 = (f32[2,8,128]{2,1,0:T(8,128)S(1)}, f32[2,8,128]{2,1,0:T(8,128)S(1)}, u32[]{:S(2)}, u32[]{:S(2)}) collective-permute-start(f32[2,8,128]{2,1,0:T(8,128)S(1)} %get-tuple-element.17), channel_id=1, source_target_pairs={{0,12},{1,13},{2,14},{3,15},{4,8},{5,9},{6,10},{7,11},{8,4},{9,5},... | collective-permute-start | bytes 24584 | tf_op jit(solution)/shard_map/ppermute | solution.py:222
  16.0 0.1 collective-permute-start.3
  16.1 0.0 collective-permute-done.4.rest_2_
  16.1 2.8 %collective-permute-done.2.rest_0_ = f32[2,8,128]{2,1,0:T(8,128)S(1)} collective-permute-done((f32[2,8,128]{2,1,0:T(8,128)S(1)}, f32[2,8,128]{2,1,0:T(8,128)S(1)}, u32[]{:S(2)}, u32[]{:S(2)}) %collective-permute-start.2) | collective-permute-done | bytes 8224 | tf_op jit(solution)/shard_map/ppermute | solution.py:222
  19.0 1.6 %collective-permute-done.3.rest_1_ = f32[2,8,128]{2,1,0:T(8,128)S(1)} collective-permute-done((f32[2,8,128]{2,1,0:T(8,128)S(1)}, f32[2,8,128]{2,1,0:T(8,128)S(1)}, u32[]{:S(2)}, u32[]{:S(2)}) %collective-permute-start.3) | collective-permute-done | bytes 8224 | tf_op jit(solution)/shard_map/ppermute | solution.py:222
  20.6 0.6 %finish.1 = (f32[2,512]{1,0:T(2,128)}, f32[1,1]{1,0:T(1,128)}) custom-call(f32[2,8,128]{2,1,0:T(8,128)S(1)} %get-tuple-element.19.own, f32[2,8,128]{2,1,0:T(8,128)S(1)} %collective-permute-done.2.rest_0_, f32[2,8,128]{2,1,0:T(8,128)S(1)} %collective-permute-done.3.rest_1_, f32[2,8,128]{2,1,0:T(8,128)S(1)} %collective-permute-done.4.rest_2_), custom_call_target="tpu_custom_call" | custom-call | tf_op jit(solution)/shard_map/finish/pallas_call | solution.py:207
  (4 shorter events, 0.0 us)
Async XLA Ops:
  4.5 1.6 %collective-permute-start = (f32[264,128]{1,0:T(8,128)S(1)}, f32[264,128]{1,0:T(8,128)S(1)}, u32[]{:S(2)}, u32[]{:S(2)}) collective-permute-start(f32[264,128]{1,0:T(8,128)S(1)} %get-tuple-element.7.own), channel_id=1, source_target_pairs={{0,1},{1,0},{2,3},{3,2},{4,5},{5,4},{6,7},{7,6},{8,9},{9,8},{10,11... | collective-permute-start | bytes 405512 | tf_op jit(solution)/shard_map/ppermute | solution.py:222
  6.6 4.7 %collective-permute-start.1 = (f32[5,8,128]{2,1,0:T(8,128)S(1)}, f32[5,8,128]{2,1,0:T(8,128)S(1)}, u32[]{:S(2)}, u32[]{:S(2)}) collective-permute-start(f32[5,8,128]{2,1,0:T(8,128)S(1)} %lookup.3), channel_id=1, source_target_pairs={{0,2},{1,3},{2,0},{3,1},{4,6},{5,7},{6,4},{7,5},{8,10},{9,11},{10,... | collective-permute-start | bytes 61448 | tf_op jit(solution)/shard_map/ppermute | solution.py:222
  11.4 4.8 %collective-permute-start.4 = (f32[2,8,128]{2,1,0:T(8,128)S(1)}, f32[2,8,128]{2,1,0:T(8,128)S(1)}, u32[]{:S(2)}, u32[]{:S(2)}) collective-permute-start(f32[2,8,128]{2,1,0:T(8,128)S(1)} %get-tuple-element.16), channel_id=1, source_target_pairs={{0,4},{1,5},{2,6},{3,7},{4,0},{5,1},{6,2},{7,3},{8,12},{9,13},{10,... | collective-permute-start | bytes 24584 | tf_op jit(solution)/shard_map/ppermute | solution.py:222
  13.5 5.4 %collective-permute-start.2 = (f32[2,8,128]{2,1,0:T(8,128)S(1)}, f32[2,8,128]{2,1,0:T(8,128)S(1)}, u32[]{:S(2)}, u32[]{:S(2)}) collective-permute-start(f32[2,8,128]{2,1,0:T(8,128)S(1)} %get-tuple-element.17), channel_id=1, source_target_pairs={{0,12},{1,13},{2,14},{3,15},{4,8},{5,9},{6,10},{7,11},{8,4},{9,5},... | collective-permute-start | bytes 24584 | tf_op jit(solution)/shard_map/ppermute | solution.py:222
  16.0 4.5 %collective-permute-start.3 = (f32[2,8,128]{2,1,0:T(8,128)S(1)}, f32[2,8,128]{2,1,0:T(8,128)S(1)}, u32[]{:S(2)}, u32[]{:S(2)}) collective-permute-start(f32[2,8,128]{2,1,0:T(8,128)S(1)} %get-tuple-element.18), channel_id=1, source_target_pairs={{0,8},{1,9},{2,10},{3,11},{4,12},{5,13},{6,14},{7,15},{8,0},{9,1},... | collective-permute-start | bytes 24584 | tf_op jit(solution)/shard_map/ppermute | solution.py:222

commit v3 on v2

--- a/solution.py
+++ b/solution.py
@@ -9,6 +9,7 @@
 
 LANES = 128
 TILE = 8
+STAGES = [(9,), (3, 5)]
 
 
 def fold(values, join):
@@ -62,6 +63,7 @@
         for part in range(2):
             for value in range(2):
                 copies[step, part, value].wait()
+        for part in range(2):
             result.append(jnp.dot(wide[step], weights[step, part], preferred_element_type=jnp.float32))
         by_real, by_imag = result
         return by_real[:block] - by_imag[block:], by_imag[:block] + by_real[block:]
@@ -137,25 +139,23 @@
     )(in_hbm(cuts.T), in_hbm(stem), in_hbm(branch), in_hbm(bit_rows), in_hbm(bit_cols))
 
 
-def lookup_kernel(rows, chunks, other, own, got, lane_of, line_of, out):
+def lookup_kernel(rows, offsets, own, got, lane_of, line_of, out):
     entries = own.shape[0] - TILE
     groups = entries // (2 * rows)
-    per_chunk = lane_of.shape[0] // (2 * chunks * 2)
     me = lax.axis_index("cuts")
-    side = (me // 2) % 2
-    which = 2 * (1 - side if other else side) + me % 2
+    per_chunk = lane_of.shape[0] // lax.axis_size("cuts")
     table = own[:entries, :] + got[:entries, :]
     high = table.astype(jnp.bfloat16)
-    low = (table - high.astype(jnp.float32)).astype(jnp.bfloat16)
-    left = jnp.concatenate([high, low], axis=1)
+    rest = (table - high.astype(jnp.float32)).astype(jnp.bfloat16)
+    left = jnp.concatenate([high, rest], axis=1)
     lane = lax.broadcasted_iota(jnp.int32, (LANES, LANES), 0)
     row = lax.broadcasted_iota(jnp.int32, (TILE, LANES), 0)
 
     def hot(line):
         return jnp.where(lane == lane_of[pl.ds(line, 1), :], 1.0, 0.0).astype(jnp.bfloat16)
 
-    for chunk in range(chunks):
-        first = (which + 4 * chunk) * per_chunk
+    for chunk, offset in enumerate(offsets):
+        first = (me ^ offset) * per_chunk
         for pair in range(0, per_chunk, 2):
             right = jnp.concatenate([hot(first + pair), hot(first + pair + 1)], axis=1)
             both = jnp.dot(left, jnp.concatenate([right, right], axis=0), preferred_element_type=jnp.float32)
@@ -171,18 +171,20 @@
                             found[part] = found[part] + jnp.where(here, values[begin : begin + TILE], 0.0)
                 for part in range(2):
                     out[chunk, pl.ds(2 * (pair + group) + part, 1), :] = jnp.sum(found[part], axis=0, keepdims=True)
-    out[chunks] = jnp.maximum(own[entries:, :], got[entries:, :])
-
-
-def lookup(rows, chunks, other, *operands):
+    out[len(offsets)] = jnp.maximum(own[entries:, :], got[entries:, :])
+
+
+def lookup(rows, offsets, *operands):
     vmem = pl.BlockSpec(memory_space=pltpu.VMEM)
     return pl.pallas_call(
-        functools.partial(lookup_kernel, rows, chunks, other),
-        out_shape=pltpu.VMEM((chunks + 1, TILE, LANES), jnp.float32),
+        functools.partial(lookup_kernel, rows, offsets),
+        out_shape=pltpu.VMEM((len(offsets) + 1, TILE, LANES), jnp.float32),
         in_specs=[vmem] * 4,
         out_specs=vmem,
         compiler_params=pltpu.CompilerParams(vmem_limit_bytes=16 << 20),
-        cost_estimate=pl.CostEstimate(flops=chunks * 2 * 512 * 256 * 256, bytes_accessed=1 << 20, transcendentals=0),
+        cost_estimate=pl.CostEstimate(
+            flops=len(offsets) * 2 * 512 * 256 * 256, bytes_accessed=1 << 20, transcendentals=0
+        ),
         name="lookup",
     )(*map(in_vmem, operands))
 
@@ -218,40 +220,60 @@
     return amplitudes, log_scale.reshape(1)
 
 
-def swap(value, bit):
-    return lax.ppermute(value, "cuts", [(i, i ^ bit) for i in range(lax.axis_size("cuts"))])
+def stages(devices):
+    if devices == 16:
+        return STAGES
+    result, bit = [], 2
+    while bit < devices:
+        result.append((bit + 1,))
+        bit *= 2
+    return result
+
+
+def span(steps):
+    found = [0]
+    for step in steps:
+        found = found + [step ^ other for other in found]
+    return found
+
+
+def nested(plan):
+    return [a ^ b for a in span(plan[0]) for b in nested(plan[1:])] if plan else [0]
+
+
+def swap(value, step):
+    return lax.ppermute(value, "cuts", [(i, i ^ step) for i in range(lax.axis_size("cuts"))])
 
 
 def merge(kept, arrived):
     return jnp.concatenate([kept[:-1] + arrived[:-1], jnp.maximum(kept[-1:], arrived[-1:])])
 
 
-def exchange(held, bit, radix):
-    mine = (lax.axis_index("cuts") // bit) % radix
-    share = (held.shape[0] - 1) // radix
-
-    def of(index):
-        return jnp.concatenate([lax.dynamic_slice_in_dim(held, index * share, share), held[-1:]])
-
-    arrived = [swap(of(mine ^ other), bit * other) for other in range(radix - 1, 0, -1)]
-    return [of(mine), *arrived]
-
-
 def shards(stem_tensor, branch_tensors, cut_values, bit_rows, bit_cols):
-    rows, width = stem_tensor.shape[2:]
-    devices = lax.axis_size("cuts")
-    half = devices // 4
+    rows = stem_tensor.shape[2]
     own, lane_of, line_of = contract(
         stem_tensor, branch_tensors, cut_values, bit_rows.reshape(-1, LANES), bit_cols.reshape(-1, LANES)
     )
     got = swap(own, 1)
-    arrived = swap(lookup(rows, half, True, own, got, lane_of, line_of), 2)
-    pieces = [lookup(rows, half, False, own, got, lane_of, line_of), arrived]
-    bit = 4
-    while bit < devices:
-        radix = 4 if bit * 4 <= devices else 2
-        pieces = exchange(functools.reduce(merge, pieces), bit, radix)
-        bit *= radix
+    plan = stages(lax.axis_size("cuts"))
+    pieces = None
+    for index, steps in enumerate(plan):
+        later = nested(plan[index + 1 :])
+        count = len(later)
+        offsets = span(steps)
+        if pieces is None:
+            parts = [
+                functools.partial(lookup, rows, [offset ^ other for other in later], own, got, lane_of, line_of)
+                for offset in offsets
+            ]
+        else:
+            held = functools.reduce(merge, pieces)
+            parts = [
+                functools.partial(lambda at, held: jnp.concatenate([held[at : at + count], held[-1:]]), n * count, held)
+                for n in range(len(offsets))
+            ]
+        arrived = [swap(part(), offset) for part, offset in reversed(list(zip(parts, offsets))[1:])]
+        pieces = [parts[0](), *arrived]
     return finish(*pieces)
 
 

time: 21.3 us -> 18.6 us (0.87)
  waiting for transfers between devices: 6.64 us -> 4.98 us
  starting transfers between devices: 8.25 us -> 7.49 us
  Pallas kernels: 5.58 us -> 5.32 us
    ppermute x5, waiting for transfers between devices: 6.64 us -> 4.98 us  [swap(): lax.ppermute(value, 'cuts', [(i, i ^ step) for i in range(lax.axis_size('...]
    ppermute x5, starting transfers between devices: 8.25 us -> 7.49 us  [swap(): lax.ppermute(value, 'cuts', [(i, i ^ step) for i in range(lax.axis_size('...]
    pallas_call x1, Pallas kernels: 3.91 us -> 3.65 us  [contract(): pl.pallas_call(contract_kernel, out_shape=(pltpu.VMEM((entries + TILE, LA...]
  transfers between devices with their start and end apart: 5 -> 5, of which waited for: 4 -> 3; matrix products, arithmetic and copies ran while one was open for 0% -> 0% of each run, Pallas kernels for 2% -> 3%
where the time goes in v3:
time: 18.6 us; the launch traced here: 18.5 us
  starting transfers between devices  7.49 us (40%)
  Pallas kernels  5.32 us (29%)
  waiting for transfers between devices  4.98 us (27%)
  between operations  0.67 us (4%)
    ppermute x5, starting transfers between devices, swap(): lax.ppermute(value, 'cuts', [(i, i ^ step) for i in range(lax.axis_size('...  7.49 us
    ppermute x5, waiting for transfers between devices, swap(): lax.ppermute(value, 'cuts', [(i, i ^ step) for i in range(lax.axis_size('...  4.98 us
    pallas_call x1, Pallas kernels, contract(): pl.pallas_call(contract_kernel, out_shape=(pltpu.VMEM((entries + TILE, LA...  3.65 us
    pallas_call x2, Pallas kernels, lookup(): pl.pallas_call(functools.partial(lookup_kernel, rows, offsets), out_shape...  1.05 us
    pallas_call x1, Pallas kernels, finish(): pl.pallas_call(finish_kernel, out_shape=(jax.ShapeDtypeStruct((2, TILE //...  0.62 us
  transfers between devices with their start and end apart: 5, of which 3 were waited for; matrix products, arithmetic and copies ran while one was open for 0% of the time, Pallas kernels for 3%

profile of v3, /device:TPU:0, one launch (start us, length us, event | category | flops | bytes accessed | tf_op | source)
XLA Modules:
  0.0 18.5 jit_solution(4454998320507377679)
XLA Ops:
  0.6 3.6 %contract.1 = (f32[264,128]{1,0:T(8,128)S(1)}, s32[64,128]{1,0:T(8,128)S(1)}, s32[64,128]{1,0:T(8,128)S(1)}) custom-call(s32[2,4]{1,0:T(2,128)} %bitcast.6, bf16[2,4,32,512]{3,2,1,0:T(8,128)(2,1)} %stem.1, bf16[2,2,2,512,512]{4,3,2,1,0:T(8,128)(2,1)} %branch.1, s32[64,128]{1,0:T(8,128)} %bitcast.4, s32[64,128]{1,0:T(8,128)} %bitcast.5), custom_call_target="tpu_custom_call" | custom-call | flops 1073741824 | bytes 4194304 | tf_op jit(solution)/shard_map/contract/pallas_call | solution.py:116
  4.3 0.6 %collective-permute-start = (f32[264,128]{1,0:T(8,128)S(1)}, f32[264,128]{1,0:T(8,128)S(1)}, u32[]{:S(2)}, u32[]{:S(2)}) collective-permute-start(f32[264,128]{1,0:T(8,128)S(1)} %get-tuple-element.7.own), channel_id=1, source_target_pairs={{0,1},{1,0},{2,3},{3,2},{4,5},{5,4},{6,7},{7,6},{8,9},{9,8},{10,11... | collective-permute-start | bytes 405512 | tf_op jit(solution)/shard_map/ppermute | solution.py:245
  4.8 1.0 %collective-permute-done.got = f32[264,128]{1,0:T(8,128)S(1)} collective-permute-done((f32[264,128]{1,0:T(8,128)S(1)}, f32[264,128]{1,0:T(8,128)S(1)}, u32[]{:S(2)}, u32[]{:S(2)}) %collective-permute-start) | collective-permute-done | bytes 135200 | tf_op jit(solution)/shard_map/ppermute | solution.py:245
  5.8 0.5 %lookup.3 = f32[5,8,128]{2,1,0:T(8,128)S(1)} custom-call(f32[264,128]{1,0:T(8,128)S(1)} %get-tuple-element.7.own, f32[264,128]{1,0:T(8,128)S(1)} %collective-permute-done.got, s32[64,128]{1,0:T(8,128)S(1)} %get-tuple-element.8.lane_of, s32[64,128]{1,0:T(8,128)S(1)} %get-tuple-element.9.line_of), custom_call_target="tpu_custom_call" | custom-call | flops 268435456 | bytes 1048576 | tf_op jit(solution)/shard_map/lookup/pallas_call | solution.py:179
  6.4 3.7 %collective-permute-start.1 = (f32[5,8,128]{2,1,0:T(8,128)S(1)}, f32[5,8,128]{2,1,0:T(8,128)S(1)}, u32[]{:S(2)}, u32[]{:S(2)}) collective-permute-start(f32[5,8,128]{2,1,0:T(8,128)S(1)} %lookup.3), channel_id=1, source_target_pairs={{0,9},{1,8},{2,11},{3,10},{4,13},{5,12},{6,15},{7,14},{8,1},{9,0},... | collective-permute-start | bytes 61448 | tf_op jit(solution)/shard_map/ppermute | solution.py:245
  10.1 0.5 %lookup.2 = f32[5,8,128]{2,1,0:T(8,128)S(1)} custom-call(f32[264,128]{1,0:T(8,128)S(1)} %get-tuple-element.7.own, f32[264,128]{1,0:T(8,128)S(1)} %collective-permute-done.got, s32[64,128]{1,0:T(8,128)S(1)} %get-tuple-element.8.lane_of, s32[64,128]{1,0:T(8,128)S(1)} %get-tuple-element.9.line_of), custom_call_target="tpu_custom_call" | custom-call | flops 268435456 | bytes 1048576 | tf_op jit(solution)/shard_map/lookup/pallas_call | solution.py:179
  10.6 1.0 %collective-permute-done.1 = f32[5,8,128]{2,1,0:T(8,128)S(1)} collective-permute-done((f32[5,8,128]{2,1,0:T(8,128)S(1)}, f32[5,8,128]{2,1,0:T(8,128)S(1)}, u32[]{:S(2)}, u32[]{:S(2)}) %collective-permute-start.1) | collective-permute-done | bytes 20512 | tf_op jit(solution)/shard_map/ppermute | solution.py:245
  11.6 1.6 %collective-permute-start.4 = (f32[2,8,128]{2,1,0:T(8,128)S(1)}, f32[2,8,128]{2,1,0:T(8,128)S(1)}, u32[]{:S(2)}, u32[]{:S(2)}) collective-permute-start(f32[2,8,128]{2,1,0:T(8,128)S(1)} %get-tuple-element.16), channel_id=1, source_target_pairs={{0,3},{1,2},{2,1},{3,0},{4,7},{5,6},{6,5},{7,4},{8,11},{9,10},{10,... | collective-permute-start | bytes 24584 | tf_op jit(solution)/shard_map/ppermute | solution.py:245
  13.3 1.5 %collective-permute-start.2 = (f32[2,8,128]{2,1,0:T(8,128)S(1)}, f32[2,8,128]{2,1,0:T(8,128)S(1)}, u32[]{:S(2)}, u32[]{:S(2)}) collective-permute-start(f32[2,8,128]{2,1,0:T(8,128)S(1)} %get-tuple-element.17), channel_id=1, source_target_pairs={{0,6},{1,7},{2,4},{3,5},{4,2},{5,3},{6,0},{7,1},{8,14},{9,15},{10,... | collective-permute-start | bytes 24584 | tf_op jit(solution)/shard_map/ppermute | solution.py:245
  14.8 0.0 collective-permute-start.3
  14.8 0.0 collective-permute-done.4.rest_2_
  14.8 3.0 %collective-permute-done.2.rest_0_ = f32[2,8,128]{2,1,0:T(8,128)S(1)} collective-permute-done((f32[2,8,128]{2,1,0:T(8,128)S(1)}, f32[2,8,128]{2,1,0:T(8,128)S(1)}, u32[]{:S(2)}, u32[]{:S(2)}) %collective-permute-start.2) | collective-permute-done | bytes 8224 | tf_op jit(solution)/shard_map/ppermute | solution.py:245
  17.8 0.0 collective-permute-done.3.rest_1_
  17.8 0.6 %finish.1 = (f32[2,512]{1,0:T(2,128)}, f32[1,1]{1,0:T(1,128)}) custom-call(f32[2,8,128]{2,1,0:T(8,128)S(1)} %get-tuple-element.19.own, f32[2,8,128]{2,1,0:T(8,128)S(1)} %collective-permute-done.2.rest_0_, f32[2,8,128]{2,1,0:T(8,128)S(1)} %collective-permute-done.3.rest_1_, f32[2,8,128]{2,1,0:T(8,128)S(1)} %collective-permute-done.4.rest_2_), custom_call_target="tpu_custom_call" | custom-call | tf_op jit(solution)/shard_map/finish/pallas_call | solution.py:209
  (3 shorter events, 0.0 us)
Async XLA Ops:
  4.3 1.6 %collective-permute-start = (f32[264,128]{1,0:T(8,128)S(1)}, f32[264,128]{1,0:T(8,128)S(1)}, u32[]{:S(2)}, u32[]{:S(2)}) collective-permute-start(f32[264,128]{1,0:T(8,128)S(1)} %get-tuple-element.7.own), channel_id=1, source_target_pairs={{0,1},{1,0},{2,3},{3,2},{4,5},{5,4},{6,7},{7,6},{8,9},{9,8},{10,11... | collective-permute-start | bytes 405512 | tf_op jit(solution)/shard_map/ppermute | solution.py:245
  6.4 5.2 %collective-permute-start.1 = (f32[5,8,128]{2,1,0:T(8,128)S(1)}, f32[5,8,128]{2,1,0:T(8,128)S(1)}, u32[]{:S(2)}, u32[]{:S(2)}) collective-permute-start(f32[5,8,128]{2,1,0:T(8,128)S(1)} %lookup.3), channel_id=1, source_target_pairs={{0,9},{1,8},{2,11},{3,10},{4,13},{5,12},{6,15},{7,14},{8,1},{9,0},... | collective-permute-start | bytes 61448 | tf_op jit(solution)/shard_map/ppermute | solution.py:245
  11.6 3.2 %collective-permute-start.4 = (f32[2,8,128]{2,1,0:T(8,128)S(1)}, f32[2,8,128]{2,1,0:T(8,128)S(1)}, u32[]{:S(2)}, u32[]{:S(2)}) collective-permute-start(f32[2,8,128]{2,1,0:T(8,128)S(1)} %get-tuple-element.16), channel_id=1, source_target_pairs={{0,3},{1,2},{2,1},{3,0},{4,7},{5,6},{6,5},{7,4},{8,11},{9,10},{10,... | collective-permute-start | bytes 24584 | tf_op jit(solution)/shard_map/ppermute | solution.py:245
  13.3 4.5 %collective-permute-start.2 = (f32[2,8,128]{2,1,0:T(8,128)S(1)}, f32[2,8,128]{2,1,0:T(8,128)S(1)}, u32[]{:S(2)}, u32[]{:S(2)}) collective-permute-start(f32[2,8,128]{2,1,0:T(8,128)S(1)} %get-tuple-element.17), channel_id=1, source_target_pairs={{0,6},{1,7},{2,4},{3,5},{4,2},{5,3},{6,0},{7,1},{8,14},{9,15},{10,... | collective-permute-start | bytes 24584 | tf_op jit(solution)/shard_map/ppermute | solution.py:245
  14.8 3.1 %collective-permute-start.3 = (f32[2,8,128]{2,1,0:T(8,128)S(1)}, f32[2,8,128]{2,1,0:T(8,128)S(1)}, u32[]{:S(2)}, u32[]{:S(2)}) collective-permute-start(f32[2,8,128]{2,1,0:T(8,128)S(1)} %get-tuple-element.18), channel_id=1, source_target_pairs={{0,5},{1,4},{2,7},{3,6},{4,1},{5,0},{6,3},{7,2},{8,13},{9,12},{10,... | collective-permute-start | bytes 24584 | tf_op jit(solution)/shard_map/ppermute | solution.py:245

commit v4 on v3

--- a/solution.py
+++ b/solution.py
@@ -6,6 +6,7 @@
 from jax.experimental import pallas as pl
 from jax.experimental.pallas import tpu as pltpu
 from jax.sharding import PartitionSpec as P
+
 
 LANES = 128
 TILE = 8
@@ -27,7 +28,6 @@
 def contract_kernel(cuts_in, stem, branch, rows_in, cols_in, out, lane_of, line_of, cuts, held, weights, wide, wanted, sems, branch_sem):
     _, slices, rows, width = held.shape
     steps = weights.shape[0]
-    block = slices * rows
     cuts_copy = pltpu.make_async_copy(cuts_in, cuts, sems.at[0])
     stem_copy = pltpu.make_async_copy(stem, held, sems.at[1])
     cuts_copy.start()
@@ -51,7 +51,7 @@
     stem_copy.wait()
 
     def place(step, part, piece, values):
-        where = slice(part * block + piece * rows, part * block + (piece + 1) * rows)
+        where = slice((piece * 2 + part) * rows, (piece * 2 + part + 1) * rows)
         chosen = cuts[step, piece]
         start = pl.multiple_of(chosen * width, width)
         other = pl.multiple_of((1 - chosen) * width, width)
@@ -59,14 +59,20 @@
         wide[step, where, pl.ds(other, width)] = jnp.zeros_like(values)
 
     def product(step):
-        result = []
         for part in range(2):
             for value in range(2):
                 copies[step, part, value].wait()
-        for part in range(2):
-            result.append(jnp.dot(wide[step], weights[step, part], preferred_element_type=jnp.float32))
-        by_real, by_imag = result
-        return by_real[:block] - by_imag[block:], by_imag[:block] + by_real[block:]
+        real_all, imag_all = [], []
+        per = max(slices // 2, 1)
+        for b in range(slices // per):
+            lhs = wide[step, b * per * 2 * rows : (b + 1) * per * 2 * rows]
+            by_real = jnp.dot(lhs, weights[step, 0], preferred_element_type=jnp.float32)
+            by_imag = jnp.dot(lhs, weights[step, 1], preferred_element_type=jnp.float32)
+            for piece in range(per):
+                re, im = slice(piece * 2 * rows, (piece * 2 + 1) * rows), slice((piece * 2 + 1) * rows, (piece * 2 + 2) * rows)
+                real_all.append(by_real[re] - by_imag[im])
+                imag_all.append(by_imag[re] + by_real[im])
+        return jnp.concatenate(real_all, axis=0), jnp.concatenate(imag_all, axis=0)
 
     for part in range(2):
         for piece in range(slices):
@@ -89,7 +95,7 @@
     real_small = real_part * inverse
     imag_small = imag_part * inverse
     square = fold(real_small * real_small + imag_small * imag_small, jnp.maximum)
-    second = jnp.sqrt(jnp.max(square, axis=(0, 1), keepdims=True)) * scale
+    second = jnp.sqrt(jnp.maximum(square[: TILE // 2], square[TILE // 2 :])) * scale
     for part, whole in enumerate((real_part, imag_part)):
         total = whole[:rows]
         for piece in range(1, slices):
@@ -97,8 +103,9 @@
         for group in range(width // LANES):
             start = (group * 2 + part) * rows
             out[start : start + rows, :] = total[:, group * LANES : (group + 1) * LANES]
-    index = lax.broadcasted_iota(jnp.int32, (TILE, LANES), 0)
-    out[2 * rows * (width // LANES) :, :] = jnp.where(index == 0, first, second)
+    end = 2 * rows * (width // LANES)
+    out[end : end + TILE // 2, :] = jnp.broadcast_to(first, second.shape)
+    out[end + TILE // 2 :, :] = second
 
 
 def in_hbm(value):
@@ -139,29 +146,52 @@
     )(in_hbm(cuts.T), in_hbm(stem), in_hbm(branch), in_hbm(bit_rows), in_hbm(bit_cols))
 
 
-def lookup_kernel(rows, offsets, own, got, lane_of, line_of, out):
+def mark_kernel(offsets, lane_of, line_of, hot, lines):
+    me = lax.axis_index("cuts")
+    lane = lax.broadcasted_iota(jnp.int32, (LANES, LANES), 0)
+    per_chunk = lines.shape[1]
+    for chunk, offset in enumerate(offsets):
+        for line in range(per_chunk):
+            at = pl.ds((me ^ offset) * per_chunk + line, 1)
+            lines[chunk, pl.ds(line, 1), :] = line_of[at, :]
+            hot[chunk, :, line * LANES : (line + 1) * LANES] = jnp.where(lane == lane_of[at, :], 1.0, 0.0).astype(
+                jnp.bfloat16
+            )
+
+
+def mark(offsets, lane_of, line_of):
+    vmem = pl.BlockSpec(memory_space=pltpu.VMEM)
+    per_chunk = lane_of.shape[0] // lax.axis_size("cuts")
+    return pl.pallas_call(
+        functools.partial(mark_kernel, offsets),
+        out_shape=(
+            pltpu.VMEM((len(offsets), LANES, per_chunk * LANES), jnp.bfloat16),
+            pltpu.VMEM((len(offsets), per_chunk, LANES), jnp.int32),
+        ),
+        in_specs=[vmem] * 2,
+        out_specs=[vmem] * 2,
+        compiler_params=pltpu.CompilerParams(vmem_limit_bytes=8 << 20),
+        cost_estimate=pl.CostEstimate(flops=100_000_000, bytes_accessed=len(offsets) << 17, transcendentals=0),
+        name="mark",
+    )(in_vmem(lane_of), in_vmem(line_of))
+
+
+def lookup_kernel(rows, at, own, got, hot, line_of, out):
     entries = own.shape[0] - TILE
     groups = entries // (2 * rows)
-    me = lax.axis_index("cuts")
-    per_chunk = lane_of.shape[0] // lax.axis_size("cuts")
+    chunks, per_chunk = out.shape[0] - 1, line_of.shape[1]
     table = own[:entries, :] + got[:entries, :]
     high = table.astype(jnp.bfloat16)
     rest = (table - high.astype(jnp.float32)).astype(jnp.bfloat16)
     left = jnp.concatenate([high, rest], axis=1)
-    lane = lax.broadcasted_iota(jnp.int32, (LANES, LANES), 0)
     row = lax.broadcasted_iota(jnp.int32, (TILE, LANES), 0)
-
-    def hot(line):
-        return jnp.where(lane == lane_of[pl.ds(line, 1), :], 1.0, 0.0).astype(jnp.bfloat16)
-
-    for chunk, offset in enumerate(offsets):
-        first = (me ^ offset) * per_chunk
+    for chunk in range(chunks):
         for pair in range(0, per_chunk, 2):
-            right = jnp.concatenate([hot(first + pair), hot(first + pair + 1)], axis=1)
+            right = hot[at + chunk, :, pair * LANES : (pair + 2) * LANES]
             both = jnp.dot(left, jnp.concatenate([right, right], axis=0), preferred_element_type=jnp.float32)
             for group in range(2):
                 values = both[:, group * LANES : (group + 1) * LANES]
-                wanted = line_of[pl.ds(first + pair + group, 1), :]
+                wanted = line_of[at + chunk, pl.ds(pair + group, 1), :]
                 found = [jnp.zeros((TILE, LANES), jnp.float32) for _ in range(2)]
                 for part_group in range(groups):
                     for start in range(0, rows, TILE):
@@ -171,19 +201,21 @@
                             found[part] = found[part] + jnp.where(here, values[begin : begin + TILE], 0.0)
                 for part in range(2):
                     out[chunk, pl.ds(2 * (pair + group) + part, 1), :] = jnp.sum(found[part], axis=0, keepdims=True)
-    out[len(offsets)] = jnp.maximum(own[entries:, :], got[entries:, :])
-
-
-def lookup(rows, offsets, *operands):
+    peaks = jnp.maximum(own[entries:, :], got[entries:, :])
+    second = jnp.max(jnp.where(row < TILE // 2, 0.0, peaks), axis=(0, 1), keepdims=True)
+    out[chunks] = jnp.where(row < TILE // 2, peaks, second)
+
+
+def lookup(rows, at, count, *operands):
     vmem = pl.BlockSpec(memory_space=pltpu.VMEM)
     return pl.pallas_call(
-        functools.partial(lookup_kernel, rows, offsets),
-        out_shape=pltpu.VMEM((len(offsets) + 1, TILE, LANES), jnp.float32),
+        functools.partial(lookup_kernel, rows, at),
+        out_shape=pltpu.VMEM((count + 1, TILE, LANES), jnp.float32),
         in_specs=[vmem] * 4,
         out_specs=vmem,
         compiler_params=pltpu.CompilerParams(vmem_limit_bytes=16 << 20),
         cost_estimate=pl.CostEstimate(
-            flops=len(offsets) * 2 * 512 * 256 * 256, bytes_accessed=1 << 20, transcendentals=0
+            flops=count * 2 * 512 * 256 * 256, bytes_accessed=1 << 20, transcendentals=0
         ),
         name="lookup",
     )(*map(in_vmem, operands))
@@ -197,7 +229,7 @@
         total = total + value[0]
         peaks = jnp.maximum(peaks, value[1])
     first = peaks[0:1] + 1e-06
-    second = peaks[1:2] / first + 1e-06
+    second = peaks[TILE - 1 :] / first + 1e-06
     total = total / first / second
     for group in range(TILE // 2):
         amplitudes[:, group * LANES : (group + 1) * LANES] = total[2 * group : 2 * group + 2]
@@ -249,22 +281,22 @@
     return jnp.concatenate([kept[:-1] + arrived[:-1], jnp.maximum(kept[-1:], arrived[-1:])])
 
 
-def shards(stem_tensor, branch_tensors, cut_values, bit_rows, bit_cols):
+def body(stem_tensor, branch_tensors, cut_values, bit_rows, bit_cols):
     rows = stem_tensor.shape[2]
+    plan = stages(lax.axis_size("cuts"))
     own, lane_of, line_of = contract(
         stem_tensor, branch_tensors, cut_values, bit_rows.reshape(-1, LANES), bit_cols.reshape(-1, LANES)
     )
     got = swap(own, 1)
-    plan = stages(lax.axis_size("cuts"))
+    hot, lines = mark(nested(plan), lane_of, line_of)
     pieces = None
     for index, steps in enumerate(plan):
-        later = nested(plan[index + 1 :])
-        count = len(later)
+        count = len(nested(plan[index + 1 :]))
         offsets = span(steps)
         if pieces is None:
             parts = [
-                functools.partial(lookup, rows, [offset ^ other for other in later], own, got, lane_of, line_of)
-                for offset in offsets
+                functools.partial(lookup, rows, n * count, count, own, got, hot, lines)
+                for n in range(len(offsets))
             ]
         else:
             held = functools.reduce(merge, pieces)
@@ -286,7 +318,7 @@
         P("grp"),
     )
     return jax.shard_map(
-        shards,
+        body,
         mesh=mesh,
         in_specs=placed,
         out_specs=(P(None, ("grp", "cuts")), P("grp")),

time: 18.6 us -> 18.3 us (0.984)
  waiting for transfers between devices: 4.98 us -> 4.52 us
    ppermute x5, waiting for transfers between devices: 4.98 us -> 4.52 us  [swap(): lax.ppermute(value, 'cuts', [(i, i ^ step) for i in range(lax.axis_size('...]
    pallas_call x2 -> x3, Pallas kernels: 1.05 us -> 1.12 us  [the longest x2 0.91 us: lookup(): pl.pallas_call(functools.partial(lookup_kernel, rows, at), out_shape=pltp...]
  transfers between devices with their start and end apart: 5 -> 5, of which waited for: 3 -> 4; matrix products, arithmetic and copies ran while one was open for 0% -> 0% of each run, Pallas kernels for 3% -> 4%
where the time goes in v4:
time: 18.3 us; the launch traced here: 18.1 us
  starting transfers between devices  7.58 us (41%)
  Pallas kernels  5.29 us (29%)
  waiting for transfers between devices  4.52 us (25%)
  between operations  0.67 us (4%)
    ppermute x5, starting transfers between devices, swap(): lax.ppermute(value, 'cuts', [(i, i ^ step) for i in range(lax.axis_size('...  7.58 us
    ppermute x5, waiting for transfers between devices, swap(): lax.ppermute(value, 'cuts', [(i, i ^ step) for i in range(lax.axis_size('...  4.52 us
    pallas_call x1, Pallas kernels, contract(): pl.pallas_call(contract_kernel, out_shape=(pltpu.VMEM((entries + TILE, LA...  3.55 us
    pallas_call x2, Pallas kernels, lookup(): pl.pallas_call(functools.partial(lookup_kernel, rows, at), out_shape=pltp...  0.91 us
    pallas_call x1, Pallas kernels, finish(): pl.pallas_call(finish_kernel, out_shape=(jax.ShapeDtypeStruct((2, TILE //...  0.62 us
  transfers between devices with their start and end apart: 5, of which 4 were waited for; matrix products, arithmetic and copies ran while one was open for 0% of the time, Pallas kernels for 4%

profile of v4, /device:TPU:0, one launch (start us, length us, event | category | flops | bytes accessed | tf_op | source)
XLA Modules:
  0.0 18.1 jit_solution(13614665578203676803)
XLA Ops:
  0.6 3.5 %contract.1 = (f32[264,128]{1,0:T(8,128)S(1)}, s32[64,128]{1,0:T(8,128)S(1)}, s32[64,128]{1,0:T(8,128)S(1)}) custom-call(s32[2,4]{1,0:T(2,128)} %bitcast.6, bf16[2,4,32,512]{3,2,1,0:T(8,128)(2,1)} %stem.1, bf16[2,2,2,512,512]{4,3,2,1,0:T(8,128)(2,1)} %branch.1, s32[64,128]{1,0:T(8,128)} %bitcast.4, s32[64,128]{1,0:T(8,128)} %bitcast.5), custom_call_target="tpu_custom_call" | custom-call | flops 1073741824 | bytes 4194304 | tf_op jit(solution)/shard_map/contract/pallas_call | solution.py:123
  4.2 0.6 %collective-permute-start = (f32[264,128]{1,0:T(8,128)S(1)}, f32[264,128]{1,0:T(8,128)S(1)}, u32[]{:S(2)}, u32[]{:S(2)}) collective-permute-start(f32[264,128]{1,0:T(8,128)S(1)} %get-tuple-element.9.own), channel_id=1, source_target_pairs={{0,1},{1,0},{2,3},{3,2},{4,5},{5,4},{6,7},{7,6},{8,9},{9,8},{10,11... | collective-permute-start | bytes 405512 | tf_op jit(solution)/shard_map/ppermute | solution.py:277
  4.7 0.2 %mark.1 = (bf16[8,128,512]{2,1,0:T(8,128)(2,1)S(1)}, s32[8,4,128]{2,1,0:T(4,128)S(1)}) custom-call(s32[64,128]{1,0:T(8,128)S(1)} %get-tuple-element.10.lane_of, s32[64,128]{1,0:T(8,128)S(1)} %get-tuple-element.11.line_of), custom_call_target="tpu_custom_call" | custom-call | flops 100000000 | bytes 1048576 | tf_op jit(solution)/shard_map/mark/pallas_call | solution.py:165
  5.0 0.8 %collective-permute-done.got = f32[264,128]{1,0:T(8,128)S(1)} collective-permute-done((f32[264,128]{1,0:T(8,128)S(1)}, f32[264,128]{1,0:T(8,128)S(1)}, u32[]{:S(2)}, u32[]{:S(2)}) %collective-permute-start) | collective-permute-done | bytes 135200 | tf_op jit(solution)/shard_map/ppermute | solution.py:277
  5.7 0.5 %lookup.3 = f32[5,8,128]{2,1,0:T(8,128)S(1)} custom-call(f32[264,128]{1,0:T(8,128)S(1)} %get-tuple-element.9.own, f32[264,128]{1,0:T(8,128)S(1)} %collective-permute-done.got, bf16[8,128,512]{2,1,0:T(8,128)(2,1)S(1)} %get-tuple-element.12.hot, s32[8,4,128]{2,1,0:T(4,128)S(1)} %get-tuple-element.13.line_of), custom_call_target="tpu_custom_call" | custom-call | flops 268435456 | bytes 1048576 | tf_op jit(solution)/shard_map/lookup/pallas_call | solution.py:211
  6.2 3.8 %collective-permute-start.1 = (f32[5,8,128]{2,1,0:T(8,128)S(1)}, f32[5,8,128]{2,1,0:T(8,128)S(1)}, u32[]{:S(2)}, u32[]{:S(2)}) collective-permute-start(f32[5,8,128]{2,1,0:T(8,128)S(1)} %lookup.3), channel_id=1, source_target_pairs={{0,9},{1,8},{2,11},{3,10},{4,13},{5,12},{6,15},{7,14},{8,1},{9,0},... | collective-permute-start | bytes 61448 | tf_op jit(solution)/shard_map/ppermute | solution.py:277
  10.0 0.5 %lookup.2 = f32[5,8,128]{2,1,0:T(8,128)S(1)} custom-call(f32[264,128]{1,0:T(8,128)S(1)} %get-tuple-element.9.own, f32[264,128]{1,0:T(8,128)S(1)} %collective-permute-done.got, bf16[8,128,512]{2,1,0:T(8,128)(2,1)S(1)} %get-tuple-element.12.hot, s32[8,4,128]{2,1,0:T(4,128)S(1)} %get-tuple-element.13.line_of), custom_call_target="tpu_custom_call" | custom-call | flops 268435456 | bytes 1048576 | tf_op jit(solution)/shard_map/lookup/pallas_call | solution.py:211
  10.4 1.0 %collective-permute-done.1 = f32[5,8,128]{2,1,0:T(8,128)S(1)} collective-permute-done((f32[5,8,128]{2,1,0:T(8,128)S(1)}, f32[5,8,128]{2,1,0:T(8,128)S(1)}, u32[]{:S(2)}, u32[]{:S(2)}) %collective-permute-start.1) | collective-permute-done | bytes 20512 | tf_op jit(solution)/shard_map/ppermute | solution.py:277
  11.5 2.9 %collective-permute-start.2 = (f32[2,8,128]{2,1,0:T(8,128)S(1)}, f32[2,8,128]{2,1,0:T(8,128)S(1)}, u32[]{:S(2)}, u32[]{:S(2)}) collective-permute-start(f32[2,8,128]{2,1,0:T(8,128)S(1)} %get-tuple-element.21), channel_id=1, source_target_pairs={{0,6},{1,7},{2,4},{3,5},{4,2},{5,3},{6,0},{7,1},{8,14},{9,15},{10,... | collective-permute-start | bytes 24584 | tf_op jit(solution)/shard_map/ppermute | solution.py:277
  14.3 0.0 collective-permute-start.3
  14.3 0.4 %collective-permute-start.4 = (f32[2,8,128]{2,1,0:T(8,128)S(1)}, f32[2,8,128]{2,1,0:T(8,128)S(1)}, u32[]{:S(2)}, u32[]{:S(2)}) collective-permute-start(f32[2,8,128]{2,1,0:T(8,128)S(1)} %get-tuple-element.20), channel_id=1, source_target_pairs={{0,3},{1,2},{2,1},{3,0},{4,7},{5,6},{6,5},{7,4},{8,11},{9,10},{10,... | collective-permute-start | bytes 24584 | tf_op jit(solution)/shard_map/ppermute | solution.py:277
  14.7 1.3 %collective-permute-done.2.rest_0_ = f32[2,8,128]{2,1,0:T(8,128)S(1)} collective-permute-done((f32[2,8,128]{2,1,0:T(8,128)S(1)}, f32[2,8,128]{2,1,0:T(8,128)S(1)}, u32[]{:S(2)}, u32[]{:S(2)}) %collective-permute-start.2) | collective-permute-done | bytes 8224 | tf_op jit(solution)/shard_map/ppermute | solution.py:277
  16.1 1.4 %collective-permute-done.3.rest_1_ = f32[2,8,128]{2,1,0:T(8,128)S(1)} collective-permute-done((f32[2,8,128]{2,1,0:T(8,128)S(1)}, f32[2,8,128]{2,1,0:T(8,128)S(1)}, u32[]{:S(2)}, u32[]{:S(2)}) %collective-permute-start.3) | collective-permute-done | bytes 8224 | tf_op jit(solution)/shard_map/ppermute | solution.py:277
  17.5 0.0 collective-permute-done.4.rest_2_
  17.5 0.6 %finish.1 = (f32[2,512]{1,0:T(2,128)}, f32[1,1]{1,0:T(1,128)}) custom-call(f32[2,8,128]{2,1,0:T(8,128)S(1)} %get-tuple-element.23.own, f32[2,8,128]{2,1,0:T(8,128)S(1)} %collective-permute-done.2.rest_0_, f32[2,8,128]{2,1,0:T(8,128)S(1)} %collective-permute-done.3.rest_1_, f32[2,8,128]{2,1,0:T(8,128)S(1)} %collective-permute-done.4.rest_2_), custom_call_target="tpu_custom_call" | custom-call | tf_op jit(solution)/shard_map/finish/pallas_call | solution.py:241
  (3 shorter events, 0.0 us)
Async XLA Ops:
  4.2 1.5 %collective-permute-start = (f32[264,128]{1,0:T(8,128)S(1)}, f32[264,128]{1,0:T(8,128)S(1)}, u32[]{:S(2)}, u32[]{:S(2)}) collective-permute-start(f32[264,128]{1,0:T(8,128)S(1)} %get-tuple-element.9.own), channel_id=1, source_target_pairs={{0,1},{1,0},{2,3},{3,2},{4,5},{5,4},{6,7},{7,6},{8,9},{9,8},{10,11... | collective-permute-start | bytes 405512 | tf_op jit(solution)/shard_map/ppermute | solution.py:277
  6.2 5.2 %collective-permute-start.1 = (f32[5,8,128]{2,1,0:T(8,128)S(1)}, f32[5,8,128]{2,1,0:T(8,128)S(1)}, u32[]{:S(2)}, u32[]{:S(2)}) collective-permute-start(f32[5,8,128]{2,1,0:T(8,128)S(1)} %lookup.3), channel_id=1, source_target_pairs={{0,9},{1,8},{2,11},{3,10},{4,13},{5,12},{6,15},{7,14},{8,1},{9,0},... | collective-permute-start | bytes 61448 | tf_op jit(solution)/shard_map/ppermute | solution.py:277
  11.5 4.6 %collective-permute-start.2 = (f32[2,8,128]{2,1,0:T(8,128)S(1)}, f32[2,8,128]{2,1,0:T(8,128)S(1)}, u32[]{:S(2)}, u32[]{:S(2)}) collective-permute-start(f32[2,8,128]{2,1,0:T(8,128)S(1)} %get-tuple-element.21), channel_id=1, source_target_pairs={{0,6},{1,7},{2,4},{3,5},{4,2},{5,3},{6,0},{7,1},{8,14},{9,15},{10,... | collective-permute-start | bytes 24584 | tf_op jit(solution)/shard_map/ppermute | solution.py:277
  14.3 3.1 %collective-permute-start.3 = (f32[2,8,128]{2,1,0:T(8,128)S(1)}, f32[2,8,128]{2,1,0:T(8,128)S(1)}, u32[]{:S(2)}, u32[]{:S(2)}) collective-permute-start(f32[2,8,128]{2,1,0:T(8,128)S(1)} %get-tuple-element.22), channel_id=1, source_target_pairs={{0,5},{1,4},{2,7},{3,6},{4,1},{5,0},{6,3},{7,2},{8,13},{9,12},{10,... | collective-permute-start | bytes 24584 | tf_op jit(solution)/shard_map/ppermute | solution.py:277
  14.3 3.1 %collective-permute-start.4 = (f32[2,8,128]{2,1,0:T(8,128)S(1)}, f32[2,8,128]{2,1,0:T(8,128)S(1)}, u32[]{:S(2)}, u32[]{:S(2)}) collective-permute-start(f32[2,8,128]{2,1,0:T(8,128)S(1)} %get-tuple-element.20), channel_id=1, source_target_pairs={{0,3},{1,2},{2,1},{3,0},{4,7},{5,6},{6,5},{7,4},{8,11},{9,10},{10,... | collective-permute-start | bytes 24584 | tf_op jit(solution)/shard_map/ppermute | solution.py:277

commit v5 on v4

--- a/solution.py
+++ b/solution.py
@@ -41,13 +41,18 @@
                     weights.at[step, part, pl.ds(value * width, width)],
                     branch_sem.at[step, part, value],
                 )
-                copy.start()
                 copies[step, part, value] = copy
+                if step == 0:
+                    copy.start()
     rows_copy = pltpu.make_async_copy(rows_in, wanted.at[0], sems.at[2])
     cols_copy = pltpu.make_async_copy(cols_in, wanted.at[1], sems.at[3])
     rows_copy.start()
     cols_copy.start()
     cuts_copy.wait()
+    for step in range(1, steps):
+        for part in range(2):
+            for value in range(2):
+                copies[step, part, value].start()
     stem_copy.wait()
 
     def place(step, part, piece, values):

time: 18.3 us -> 18.1 us (0.989)
  no operation moved by 1% of the time
where the time goes in v5:
time: 18.1 us; the launch traced here: 17.9 us
  starting transfers between devices  7.58 us (42%)
  Pallas kernels  5.13 us (28%)
  waiting for transfers between devices  4.52 us (25%)
  between operations  0.67 us (4%)
    ppermute x5, starting transfers between devices, swap(): lax.ppermute(value, 'cuts', [(i, i ^ step) for i in range(lax.axis_size('...  7.58 us
    ppermute x5, waiting for transfers between devices, swap(): lax.ppermute(value, 'cuts', [(i, i ^ step) for i in range(lax.axis_size('...  4.52 us
    pallas_call x1, Pallas kernels, contract(): pl.pallas_call(contract_kernel, out_shape=(pltpu.VMEM((entries + TILE, LA...  3.38 us
    pallas_call x2, Pallas kernels, lookup(): pl.pallas_call(functools.partial(lookup_kernel, rows, at), out_shape=pltp...  0.91 us
    pallas_call x1, Pallas kernels, finish(): pl.pallas_call(finish_kernel, out_shape=(jax.ShapeDtypeStruct((2, TILE //...  0.62 us
  transfers between devices with their start and end apart: 5, of which 4 were waited for; matrix products, arithmetic and copies ran while one was open for 0% of the time, Pallas kernels for 4%

profile of v5, /device:TPU:0, one launch (start us, length us, event | category | flops | bytes accessed | tf_op | source)
XLA Modules:
  0.0 17.9 jit_solution(2903542112922311307)
XLA Ops:
  0.6 3.4 %contract.1 = (f32[264,128]{1,0:T(8,128)S(1)}, s32[64,128]{1,0:T(8,128)S(1)}, s32[64,128]{1,0:T(8,128)S(1)}) custom-call(s32[2,4]{1,0:T(2,128)} %bitcast.6, bf16[2,4,32,512]{3,2,1,0:T(8,128)(2,1)} %stem.1, bf16[2,2,2,512,512]{4,3,2,1,0:T(8,128)(2,1)} %branch.1, s32[64,128]{1,0:T(8,128)} %bitcast.4, s32[64,128]{1,0:T(8,128)} %bitcast.5), custom_call_target="tpu_custom_call" | custom-call | flops 1073741824 | bytes 4194304 | tf_op jit(solution)/shard_map/contract/pallas_call | solution.py:128
  4.0 0.6 %collective-permute-start = (f32[264,128]{1,0:T(8,128)S(1)}, f32[264,128]{1,0:T(8,128)S(1)}, u32[]{:S(2)}, u32[]{:S(2)}) collective-permute-start(f32[264,128]{1,0:T(8,128)S(1)} %get-tuple-element.9.own), channel_id=1, source_target_pairs={{0,1},{1,0},{2,3},{3,2},{4,5},{5,4},{6,7},{7,6},{8,9},{9,8},{10,11... | collective-permute-start | bytes 405512 | tf_op jit(solution)/shard_map/ppermute | solution.py:282
  4.6 0.2 %mark.1 = (bf16[8,128,512]{2,1,0:T(8,128)(2,1)S(1)}, s32[8,4,128]{2,1,0:T(4,128)S(1)}) custom-call(s32[64,128]{1,0:T(8,128)S(1)} %get-tuple-element.10.lane_of, s32[64,128]{1,0:T(8,128)S(1)} %get-tuple-element.11.line_of), custom_call_target="tpu_custom_call" | custom-call | flops 100000000 | bytes 1048576 | tf_op jit(solution)/shard_map/mark/pallas_call | solution.py:170
  4.8 0.8 %collective-permute-done.got = f32[264,128]{1,0:T(8,128)S(1)} collective-permute-done((f32[264,128]{1,0:T(8,128)S(1)}, f32[264,128]{1,0:T(8,128)S(1)}, u32[]{:S(2)}, u32[]{:S(2)}) %collective-permute-start) | collective-permute-done | bytes 135200 | tf_op jit(solution)/shard_map/ppermute | solution.py:282
  5.6 0.5 %lookup.3 = f32[5,8,128]{2,1,0:T(8,128)S(1)} custom-call(f32[264,128]{1,0:T(8,128)S(1)} %get-tuple-element.9.own, f32[264,128]{1,0:T(8,128)S(1)} %collective-permute-done.got, bf16[8,128,512]{2,1,0:T(8,128)(2,1)S(1)} %get-tuple-element.12.hot, s32[8,4,128]{2,1,0:T(4,128)S(1)} %get-tuple-element.13.line_of), custom_call_target="tpu_custom_call" | custom-call | flops 268435456 | bytes 1048576 | tf_op jit(solution)/shard_map/lookup/pallas_call | solution.py:216
  6.0 3.8 %collective-permute-start.1 = (f32[5,8,128]{2,1,0:T(8,128)S(1)}, f32[5,8,128]{2,1,0:T(8,128)S(1)}, u32[]{:S(2)}, u32[]{:S(2)}) collective-permute-start(f32[5,8,128]{2,1,0:T(8,128)S(1)} %lookup.3), channel_id=1, source_target_pairs={{0,9},{1,8},{2,11},{3,10},{4,13},{5,12},{6,15},{7,14},{8,1},{9,0},... | collective-permute-start | bytes 61448 | tf_op jit(solution)/shard_map/ppermute | solution.py:282
  9.8 0.5 %lookup.2 = f32[5,8,128]{2,1,0:T(8,128)S(1)} custom-call(f32[264,128]{1,0:T(8,128)S(1)} %get-tuple-element.9.own, f32[264,128]{1,0:T(8,128)S(1)} %collective-permute-done.got, bf16[8,128,512]{2,1,0:T(8,128)(2,1)S(1)} %get-tuple-element.12.hot, s32[8,4,128]{2,1,0:T(4,128)S(1)} %get-tuple-element.13.line_of), custom_call_target="tpu_custom_call" | custom-call | flops 268435456 | bytes 1048576 | tf_op jit(solution)/shard_map/lookup/pallas_call | solution.py:216
  10.2 1.0 %collective-permute-done.1 = f32[5,8,128]{2,1,0:T(8,128)S(1)} collective-permute-done((f32[5,8,128]{2,1,0:T(8,128)S(1)}, f32[5,8,128]{2,1,0:T(8,128)S(1)}, u32[]{:S(2)}, u32[]{:S(2)}) %collective-permute-start.1) | collective-permute-done | bytes 20512 | tf_op jit(solution)/shard_map/ppermute | solution.py:282
  11.3 2.9 %collective-permute-start.2 = (f32[2,8,128]{2,1,0:T(8,128)S(1)}, f32[2,8,128]{2,1,0:T(8,128)S(1)}, u32[]{:S(2)}, u32[]{:S(2)}) collective-permute-start(f32[2,8,128]{2,1,0:T(8,128)S(1)} %get-tuple-element.21), channel_id=1, source_target_pairs={{0,6},{1,7},{2,4},{3,5},{4,2},{5,3},{6,0},{7,1},{8,14},{9,15},{10,... | collective-permute-start | bytes 24584 | tf_op jit(solution)/shard_map/ppermute | solution.py:282
  14.2 0.0 collective-permute-start.3
  14.2 0.4 %collective-permute-start.4 = (f32[2,8,128]{2,1,0:T(8,128)S(1)}, f32[2,8,128]{2,1,0:T(8,128)S(1)}, u32[]{:S(2)}, u32[]{:S(2)}) collective-permute-start(f32[2,8,128]{2,1,0:T(8,128)S(1)} %get-tuple-element.20), channel_id=1, source_target_pairs={{0,3},{1,2},{2,1},{3,0},{4,7},{5,6},{6,5},{7,4},{8,11},{9,10},{10,... | collective-permute-start | bytes 24584 | tf_op jit(solution)/shard_map/ppermute | solution.py:282
  14.6 1.3 %collective-permute-done.2.rest_0_ = f32[2,8,128]{2,1,0:T(8,128)S(1)} collective-permute-done((f32[2,8,128]{2,1,0:T(8,128)S(1)}, f32[2,8,128]{2,1,0:T(8,128)S(1)}, u32[]{:S(2)}, u32[]{:S(2)}) %collective-permute-start.2) | collective-permute-done | bytes 8224 | tf_op jit(solution)/shard_map/ppermute | solution.py:282
  15.9 1.4 %collective-permute-done.3.rest_1_ = f32[2,8,128]{2,1,0:T(8,128)S(1)} collective-permute-done((f32[2,8,128]{2,1,0:T(8,128)S(1)}, f32[2,8,128]{2,1,0:T(8,128)S(1)}, u32[]{:S(2)}, u32[]{:S(2)}) %collective-permute-start.3) | collective-permute-done | bytes 8224 | tf_op jit(solution)/shard_map/ppermute | solution.py:282
  17.3 0.0 collective-permute-done.4.rest_2_
  17.3 0.6 %finish.1 = (f32[2,512]{1,0:T(2,128)}, f32[1,1]{1,0:T(1,128)}) custom-call(f32[2,8,128]{2,1,0:T(8,128)S(1)} %get-tuple-element.23.own, f32[2,8,128]{2,1,0:T(8,128)S(1)} %collective-permute-done.2.rest_0_, f32[2,8,128]{2,1,0:T(8,128)S(1)} %collective-permute-done.3.rest_1_, f32[2,8,128]{2,1,0:T(8,128)S(1)} %collective-permute-done.4.rest_2_), custom_call_target="tpu_custom_call" | custom-call | tf_op jit(solution)/shard_map/finish/pallas_call | solution.py:246
  (3 shorter events, 0.0 us)
Async XLA Ops:
  4.0 1.6 %collective-permute-start = (f32[264,128]{1,0:T(8,128)S(1)}, f32[264,128]{1,0:T(8,128)S(1)}, u32[]{:S(2)}, u32[]{:S(2)}) collective-permute-start(f32[264,128]{1,0:T(8,128)S(1)} %get-tuple-element.9.own), channel_id=1, source_target_pairs={{0,1},{1,0},{2,3},{3,2},{4,5},{5,4},{6,7},{7,6},{8,9},{9,8},{10,11... | collective-permute-start | bytes 405512 | tf_op jit(solution)/shard_map/ppermute | solution.py:282
  6.0 5.2 %collective-permute-start.1 = (f32[5,8,128]{2,1,0:T(8,128)S(1)}, f32[5,8,128]{2,1,0:T(8,128)S(1)}, u32[]{:S(2)}, u32[]{:S(2)}) collective-permute-start(f32[5,8,128]{2,1,0:T(8,128)S(1)} %lookup.3), channel_id=1, source_target_pairs={{0,9},{1,8},{2,11},{3,10},{4,13},{5,12},{6,15},{7,14},{8,1},{9,0},... | collective-permute-start | bytes 61448 | tf_op jit(solution)/shard_map/ppermute | solution.py:282
  11.3 4.6 %collective-permute-start.2 = (f32[2,8,128]{2,1,0:T(8,128)S(1)}, f32[2,8,128]{2,1,0:T(8,128)S(1)}, u32[]{:S(2)}, u32[]{:S(2)}) collective-permute-start(f32[2,8,128]{2,1,0:T(8,128)S(1)} %get-tuple-element.21), channel_id=1, source_target_pairs={{0,6},{1,7},{2,4},{3,5},{4,2},{5,3},{6,0},{7,1},{8,14},{9,15},{10,... | collective-permute-start | bytes 24584 | tf_op jit(solution)/shard_map/ppermute | solution.py:282
  14.2 3.1 %collective-permute-start.3 = (f32[2,8,128]{2,1,0:T(8,128)S(1)}, f32[2,8,128]{2,1,0:T(8,128)S(1)}, u32[]{:S(2)}, u32[]{:S(2)}) collective-permute-start(f32[2,8,128]{2,1,0:T(8,128)S(1)} %get-tuple-element.22), channel_id=1, source_target_pairs={{0,5},{1,4},{2,7},{3,6},{4,1},{5,0},{6,3},{7,2},{8,13},{9,12},{10,... | collective-permute-start | bytes 24584 | tf_op jit(solution)/shard_map/ppermute | solution.py:282
  14.2 3.1 %collective-permute-start.4 = (f32[2,8,128]{2,1,0:T(8,128)S(1)}, f32[2,8,128]{2,1,0:T(8,128)S(1)}, u32[]{:S(2)}, u32[]{:S(2)}) collective-permute-start(f32[2,8,128]{2,1,0:T(8,128)S(1)} %get-tuple-element.20), channel_id=1, source_target_pairs={{0,3},{1,2},{2,1},{3,0},{4,7},{5,6},{6,5},{7,4},{8,11},{9,10},{10,... | collective-permute-start | bytes 24584 | tf_op jit(solution)/shard_map/ppermute | solution.py:282
